TPU v7x, 256 devices: a whole 4x4x8 slice. The times are simulated.
256 devices in a mesh: dp: 32 (over y, z), rows: 8 (over x, core).
Axes of the slice: x: 4, y: 4, z: 8, core: 2. Of those that a mesh axis runs over, the one named last changes fastest.
Arguments:
- real_frames: bfloat16 [32, 3, 128, 256], P('dp', None, 'rows'), may hold values from -4 to 4
- fake_frames: bfloat16 [32, 3, 128, 256], P('dp', None, 'rows'), may hold values from -4 to 4
- conv_one: bfloat16 [3, 3, 3, 64], replicated, may hold values from -1.25 to 1.25
- conv_two: bfloat16 [3, 3, 64, 128], replicated, may hold values from -0.25 to 0.25
- conv_three: bfloat16 [3, 3, 128, 256], replicated, may hold values from -0.1875 to 0.1875
- conv_four: bfloat16 [3, 3, 256, 512], replicated, may hold values from -0.125 to 0.125
- conv_five: bfloat16 [3, 3, 512, 512], replicated, may hold values from -0.09375 to 0.09375
- bias_one: float32 [64], replicated, may hold values from -2 to 2
- bias_two: float32 [128], replicated, may hold values from -2 to 2
- bias_three: float32 [256], replicated, may hold values from -2 to 2
- bias_four: float32 [512], replicated, may hold values from -2 to 2
- bias_five: float32 [512], replicated, may hold values from -2 to 2
- linear_one: float32 [64], replicated, may hold values from 0.05 to 2
- linear_two: float32 [128], replicated, may hold values from 0.05 to 2
- linear_three: float32 [256], replicated, may hold values from 0.05 to 2
- linear_four: float32 [512], replicated, may hold values from 0.05 to 2
- linear_five: float32 [512], replicated, may hold values from 0.25 to 10
Outputs:
- tap_losses: float32 [5], replicated
- fake_grad: float32 [32, 3, 128, 256], P('dp', None, 'rows')
All inputs are finite; a program needn't handle non-finite values.
Results may differ from a plain program's by a relative error of at most 0.0065.
Values may be sent and summed in bfloat16 or wider, within the bound.
A program may use at most 128 MiB of HBM per device.

v0:
```python
import functools

import jax
import jax.numpy as jnp
from jax import lax
from jax.experimental import pallas as pl
from jax.experimental.pallas import tpu as pltpu
from jax.sharding import PartitionSpec as P

MESH = pl.DeviceIdType.MESH
F32 = jnp.float32
BF = jnp.bfloat16
EPS = 1e-06
ROOT = 0.7978845608028654
CUBE = 0.044715

ROWS = 8
NZ = 8
NY = 4


def dot(a, b):
    return lax.dot_general(a, b, (((1,), (0,)), ((), ())), preferred_element_type=F32)


def dot_t(a, b):
    return lax.dot_general(a, b, (((1,), (1,)), ((), ())), preferred_element_type=F32)


def iota(shape, dim):
    return lax.broadcasted_iota(jnp.int32, shape, dim)


def onehot(cond):
    return jnp.where(cond, 1.0, 0.0).astype(BF)


def rounded(x):
    return x.astype(BF).astype(F32)


def gelu(x):
    t = jnp.tanh(x * (ROOT + (ROOT * CUBE) * (x * x)))
    return x * (0.5 + 0.5 * t)


def gelu_both(x):
    x2 = x * x
    t = jnp.tanh(x * (ROOT + (ROOT * CUBE) * x2))
    h = 0.5 + 0.5 * t
    slope = h + (0.5 * x) * (1.0 - t * t) * (ROOT + (3.0 * ROOT * CUBE) * x2)
    return x * h, slope


def tap(r, f, lin, total):
    a = lax.rsqrt(total(r * r) + EPS)
    b = lax.rsqrt(total(f * f) + EPS)
    nf = f * b
    d = r * a - nf
    ld = lin * d
    grad = (ld - nf * total(nf * ld)) * (-2.0 * b)
    return ld * d, grad


def lane_sum(x):
    return jnp.sum(x, axis=-1, keepdims=True)


def fold(x):
    m, c = x.shape
    y = jnp.sum(x.reshape(m // 8, 8, c), axis=0)
    out = y[:, 0:128]
    for j in range(1, c // 128):
        out = out + y[:, j * 128 : (j + 1) * 128]
    return out


def shifted(v, phases):
    c = v.shape[-1]
    q = iota((16, c), 0)
    n = phases * 16
    tail = jnp.where(q < 15, pltpu.roll(v[0:16], 15, 0), 0.0)
    head = jnp.where(q > 0, pltpu.roll(v[n - 16 : n], 1, 0), 0.0)
    if phases == 1:
        return head, tail
    left = jnp.concatenate([head, v[0 : n - 16]], axis=0)
    right = jnp.concatenate([v[16:n], tail], axis=0)
    return left, right


def pool_cols(v, phases):
    c = v.shape[-1]
    return jnp.sum(v.reshape(phases // 2, 2, 16, c), axis=1).reshape(phases * 8, c)


def spread_cols(v, phases):
    c = v.shape[-1]
    y = jnp.broadcast_to(v.reshape(phases, 1, 16, c), (phases, 2, 16, c))
    return y.reshape(phases * 32, c)


def body(
    real_ref, fake_ref, w1_ref, w2_hbm, w3_hbm, w4_hbm, w5_hbm,
    b1_ref, b2_ref, b3_ref, b4_ref, b5_ref, l1_ref, l2_ref, l3_ref, l4_ref, l5_ref,
    loss_ref, grad_ref,
    w2s, w2t, w3s, w4s, w5s, wsm, wb, vec, tt,
    x2, x3, x4, x5, g2, g3, g4, g5, gp1,
    a1, s1, a2, s2, a3, s3, a4, s4,
    stage0, land0, stage2, land2, stage3, land3, stage4, land4, land5, stage5,
    bs4, bl4, bs3, bl3, bs2, bl2, bs1, bl1,
    parts, own, lrow, lz, ly,
    wsem, ssem, rsem, gsend, grecv, lsend, lrecv,
):
    dp = lax.axis_index("dp")
    me = lax.axis_index("rows")
    zi = lax.rem(dp, NZ)
    yi = lax.div(dp, NZ)

    def row_peer(k):
        return (dp, lax.rem(me + k, ROWS))

    def z_peer(k):
        return (yi * NZ + lax.rem(zi + k, NZ), me)

    def y_peer(k):
        return (lax.rem(yi + k, NY) * NZ + zi, me)

    cw2 = [
        pltpu.make_async_copy(
            w2_hbm.at[pl.ds(ky * 192, 192)], w2s.at[ky, pl.ds(0, 192)], wsem.at[ky]
        )
        for ky in range(3)
    ]
    cw3 = pltpu.make_async_copy(w3_hbm, w3s, wsem.at[3])
    cw4 = pltpu.make_async_copy(w4_hbm, w4s, wsem.at[4])
    cw5 = pltpu.make_async_copy(w5_hbm, w5s, wsem.at[5])
    for c in cw2 + [cw3, cw4, cw5]:
        c.start()

    barrier = pltpu.get_barrier_semaphore()
    peers = (
        [row_peer(k) for k in range(1, ROWS)]
        + [z_peer(k) for k in range(1, NZ)]
        + [y_peer(k) for k in range(1, NY)]
    )
    for peer in peers:
        pl.semaphore_signal(barrier, inc=1, device_id=peer, device_id_type=MESH)

    def beside(stage, land, n):
        up = pltpu.make_async_remote_copy(
            src_ref=stage.at[0], dst_ref=land.at[1], send_sem=ssem.at[n, 0],
            recv_sem=rsem.at[n, 1], device_id=row_peer(ROWS - 1), device_id_type=MESH,
        )
        down = pltpu.make_async_remote_copy(
            src_ref=stage.at[1], dst_ref=land.at[0], send_sem=ssem.at[n, 1],
            recv_sem=rsem.at[n, 0], device_id=row_peer(1), device_id_type=MESH,
        )
        return up, down

    def landed(land):
        top = jnp.where(me > 0, land[0].astype(F32), 0.0)
        bottom = jnp.where(me < ROWS - 1, land[1].astype(F32), 0.0)
        return top, bottom

    images = jnp.concatenate(
        [real_ref[0].reshape(48, 256), fake_ref[0].reshape(48, 256)], axis=0
    )
    for side, row in ((0, 0), (1, 15)):
        pick = onehot(iota((16, 96), 1) == iota((16, 96), 0) * 16 + row)
        stage0[side] = dot(pick, images).astype(BF)
    pl.semaphore_wait(barrier, len(peers))
    c0 = beside(stage0, land0, 0)
    for c in c0:
        c.start()

    wsm[...] = jnp.zeros_like(wsm)
    for ky in range(3):
        for kx in range(3):
            piece = w1_ref[ky, kx].astype(F32)
            for p in range(2):
                lane = (kx + p) * 128 + p * 64
                wsm[ky * 3 : ky * 3 + 3, lane : lane + 64] = piece
    small = wsm[...].astype(BF)

    def band(rr, carry):
        idx = iota((64, 16), 0)
        k = iota((64, 16), 1)
        ky = jnp.where(k >= 3, 1, 0) + jnp.where(k >= 6, 1, 0)
        ci = k - 3 * ky
        inner = (idx >> 4 == ci) & ((idx & 15) == rr + ky - 2) & (idx < 48)
        above = (idx - 48 == ci) & (rr + ky - 2 == -1)
        below = (idx - 51 == ci) & (rr + ky - 2 == 16)
        pick = onehot((inner | above | below) & (k < 9))
        block = dot(pick, small).astype(BF)
        for d in range(4):
            wb[rr, d * 64 : (d + 1) * 64, :] = block[:, d * 128 : (d + 1) * 128]
        return carry

    lax.fori_loop(0, 18, band, 0)

    for row, ref in ((0, b1_ref), (1, l1_ref)):
        vec[row : row + 1, 0:64] = ref[...]
        vec[row : row + 1, 64:128] = ref[...]
    ones_half = onehot(iota((128, 128), 0) >> 6 == iota((128, 128), 1) >> 6)
    ones_full = jnp.full((128, 128), 1.0, BF)

    def sum_half(x):
        return dot(x.astype(BF), ones_half)

    def sum_full(x):
        return dot(x.astype(BF), ones_full)

    parts[...] = jnp.zeros_like(parts)
    w2s[:, 192:256, :] = jnp.zeros((3, 64, 128), BF)

    for c in c0:
        c.wait()
    pos = iota((128, 256), 0)
    col = iota((128, 256), 1)
    base = 16 * (pos & 15) + 2 * (pos >> 4)
    take = onehot(col == base)
    edges = jnp.concatenate([land0[0], land0[1]], axis=0)
    for i, ref in ((0, real_ref), (1, fake_ref)):
        j = iota((16, 32), 0)
        k = iota((16, 32), 1)
        top = (j < 3) & (k == 3 * i + j) & (me > 0)
        bottom = (j >= 3) & (j < 6) & (k == 16 + 3 * i + j - 3) & (me < ROWS - 1)
        halo = dot(onehot(top | bottom), edges)
        whole = jnp.concatenate([ref[0].reshape(48, 256).astype(F32), halo], axis=0)
        cols = iota((64, 256), 1)
        turned = []
        for d in range(4):
            dx = d - 1
            moved = whole if dx == 0 else pltpu.roll(whole, (-dx) % 256, 1)
            moved = jnp.where((cols + dx >= 0) & (cols + dx < 256), moved, 0.0)
            turned.append(moved.astype(BF))
        tt[i] = dot_t(take, jnp.concatenate(turned, axis=0)).astype(BF)

    lane = iota((128, 128), 1)

    def put2(row, v_r, v_f):
        for i, v in ((0, v_r), (1, v_f)):
            left, right = shifted(v, 8)
            x2[i, row, :, 0:128] = jnp.where(lane < 64, left, v).astype(BF)
            x2[i, row, :, 128:256] = right.astype(BF)

    def segment1(k, message):
        bias = vec[0:1, :]
        lin = vec[1:2, :]
        sums = [0.0, 0.0]
        for i in range(2):
            weights = wb[2 * k + i + 1]
            act_r = rounded(gelu(dot(tt[0], weights) + bias))
            act_f, slope = gelu_both(dot(tt[1], weights) + bias)
            act_f = rounded(act_f)
            terms, grad = tap(act_r, act_f, lin, sum_half)
            parts[0] += fold(terms)
            a1[2 * k + i] = slope * grad
            s1[2 * k + i] = slope * 0.25
            sums[0] = sums[0] + act_r
            sums[1] = sums[1] + act_f
        v_r, v_f = [rounded((s + pltpu.roll(s, 64, 1)) * 0.25) for s in sums]
        put2(k + 1, v_r, v_f)
        if message is not None:
            stage2[message] = jnp.where(lane < 64, v_r, v_f).astype(BF)

    segment1(0, 0)
    segment1(7, 1)
    c2 = beside(stage2, land2, 1)
    for c in c2:
        c.start()

    def inner1(k, carry):
        segment1(k, None)
        return carry

    lax.fori_loop(1, 7, inner1, 0)

    for c in cw2:
        c.wait()
    for ky in range(3):
        for kx in range(3):
            piece = w2s[ky, kx * 64 : (kx + 1) * 64, :]
            w2t[ky, 0:64, kx * 128 : (kx + 1) * 128] = piece
            w2t[ky, 64:128, kx * 128 : (kx + 1) * 128] = piece
    for c in c2:
        c.wait()
    for row, v in zip((0, 9), landed(land2)):
        other = pltpu.roll(v, 64, 1)
        put2(row, jnp.where(lane < 64, v, other), jnp.where(lane < 64, other, v))

    def put(ref, i, row, v, phases, c):
        left, right = shifted(v, phases)
        ref[i, row, :, 0:c] = left.astype(BF)
        ref[i, row, :, c : 2 * c] = v.astype(BF)
        ref[i, row, :, 2 * c : 3 * c] = right.astype(BF)

    def segment2(k, message):
        acts = []
        for i in range(2):
            pre = b2_ref[...]
            for ky in range(3):
                rows = x2[i, pl.ds(2 * k + ky, 2)].reshape(256, 256)
                pre = pre + dot(rows, w2s[ky])
            if i == 0:
                acts.append(rounded(gelu(pre)))
            else:
                act, slope = gelu_both(pre)
                acts.append(rounded(act))
        terms, grad = tap(acts[0], acts[1], l2_ref[...], sum_full)
        parts[1] += fold(terms)
        a2[pl.ds(2 * k, 2)] = (slope * (4.0 * grad)).reshape(2, 128, 128)
        s2[pl.ds(2 * k, 2)] = (slope * 0.25).reshape(2, 128, 128)
        for i in range(2):
            v = rounded(pool_cols(acts[i][0:128] + acts[i][128:256], 8) * 0.25)
            put(x3, i, k + 1, v, 4, 128)
            if message is not None:
                stage3[message, :, i * 128 : (i + 1) * 128] = v.astype(BF)

    segment2(0, 0)
    segment2(3, 1)
    c3 = beside(stage3, land3, 2)
    for c in c3:
        c.start()

    def inner2(k, carry):
        segment2(k, None)
        return carry

    lax.fori_loop(1, 3, inner2, 0)

    cw3.wait()
    for c in c3:
        c.wait()
    for row, v in zip((0, 5), landed(land3)):
        for i in range(2):
            put(x3, i, row, v[:, i * 128 : (i + 1) * 128], 4, 128)
    kept3 = []
    for k in range(2):
        pre = b3_ref[...]
        for ky in range(3):
            rows = x3[:, 2 * k + ky : 2 * k + ky + 2].reshape(256, 384)
            pre = pre + dot(rows, w3s[ky * 384 : (ky + 1) * 384, :])
        act_r = rounded(gelu(pre[0:128]))
        act_f, slope = gelu_both(pre[128:256])
        act_f = rounded(act_f)
        for i, act in ((0, act_r), (1, act_f)):
            v = rounded(pool_cols(act[0:64] + act[64:128], 4) * 0.25)
            put(x4, i, k + 1, v, 2, 256)
            stage4[k, :, i * 256 : (i + 1) * 256] = v.astype(BF)
        kept3.append((act_r, act_f, slope))
    c4 = beside(stage4, land4, 3)
    for c in c4:
        c.start()
    for k, (act_r, act_f, slope) in enumerate(kept3):
        terms, grad = tap(act_r, act_f, l3_ref[...], lane_sum)
        parts[2] += fold(terms)
        a3[2 * k : 2 * k + 2] = (slope * (16.0 * grad)).reshape(2, 64, 256)
        s3[2 * k : 2 * k + 2] = (slope * 0.25).reshape(2, 64, 256)

    cw4.wait()
    for c in c4:
        c.wait()
    for row, v in zip((0, 3), landed(land4)):
        for i in range(2):
            put(x4, i, row, v[:, i * 256 : (i + 1) * 256], 2, 256)
    pre = b4_ref[...]
    for ky in range(3):
        rows = x4[:, ky : ky + 2].reshape(128, 768)
        pre = pre + dot(rows, w4s[ky * 768 : (ky + 1) * 768, :])
    act_r = rounded(gelu(pre[0:64]))
    act_f, slope = gelu_both(pre[64:128])
    act_f = rounded(act_f)
    for i, act in ((0, act_r), (1, act_f)):
        v = pool_cols(act[0:32] + act[32:64], 2) * 0.25
        stage5[:, i * 512 : (i + 1) * 512] = v.astype(BF)
    c5 = [
        pltpu.make_async_remote_copy(
            src_ref=stage5, dst_ref=land5.at[me], send_sem=gsend.at[k - 1],
            recv_sem=grecv.at[k - 1], device_id=row_peer(k), device_id_type=MESH,
        )
        for k in range(1, ROWS)
    ]
    for c in c5:
        c.start()
    land5[me] = stage5[...]
    terms, grad = tap(act_r, act_f, l4_ref[...], lane_sum)
    parts[3] += fold(terms)
    a4[...] = (slope * (64.0 * grad)).reshape(2, 32, 512)
    s4[...] = (slope * 0.25).reshape(2, 32, 512)

    zero_row = jnp.zeros((16, 1536), BF)
    for row in (0, 9):
        x5[0, row] = zero_row
        x5[1, row] = zero_row
        g5[row] = zero_row
    cw5.wait()
    for c in c5:
        c.wait()

    def fill5(row, carry):
        v = land5[row].astype(F32)
        for i in range(2):
            put(x5, i, row + 1, v[:, i * 512 : (i + 1) * 512], 1, 512)
        return carry

    lax.fori_loop(0, ROWS, fill5, 0)
    pre = b5_ref[...]
    for ky in range(3):
        rows = x5[:, ky : ky + 8].reshape(256, 1536)
        pre = pre + dot(rows, w5s[ky * 1536 : (ky + 1) * 1536, :])
    act_r = rounded(gelu(pre[0:128]))
    act_f, slope = gelu_both(pre[128:256])
    act_f = rounded(act_f)
    terms, grad = tap(act_r, act_f, l5_ref[...], lane_sum)
    parts[4] += fold(terms) * 0.125
    gpre = rounded(slope * (256.0 * grad))

    def put_back(ref, row, v, phases, c):
        left, right = shifted(v, phases)
        ref[row, :, 0:c] = right.astype(BF)
        ref[row, :, c : 2 * c] = v.astype(BF)
        ref[row, :, 2 * c : 3 * c] = left.astype(BF)

    for row in range(ROWS):
        put_back(g5, row + 1, gpre[row * 16 : (row + 1) * 16], 1, 512)

    def spread_loss(src, land, slot, peer, count, first):
        copies = [
            pltpu.make_async_remote_copy(
                src_ref=src, dst_ref=land.at[slot], send_sem=lsend.at[first + k],
                recv_sem=lrecv.at[first + k], device_id=peer(k), device_id_type=MESH,
            )
            for k in range(1, count)
        ]
        for c in copies:
            c.start()
        land[slot] = src[...]
        return copies

    def gathered_loss(copies, land, count):
        for c in copies:
            c.wait()
        total = land[0]
        for j in range(1, count):
            total = total + land[j]
        return total

    rows_of = iota((8, 128), 0)
    mine = jnp.zeros((8, 128), F32)
    for s in range(5):
        mine = mine + jnp.where(rows_of == s, jnp.sum(parts[s], axis=0, keepdims=True), 0.0)
    own[0] = mine
    cl = spread_loss(own.at[0], lrow, me, row_peer, ROWS, 0)

    gin = jnp.zeros((16, 512), F32)
    for ky in range(3):
        rows = g5[me + 2 - ky]
        for kx in range(3):
            n = (ky * 3 + kx) * 512
            gin = gin + dot_t(rows[:, kx * 512 : (kx + 1) * 512], w5s[n : n + 512, :])

    wide = spread_cols(gin, 1)
    for j in range(2):
        v = rounded(a4[j] + s4[j] * wide)
        bs4[j] = v.astype(BF)
        put_back(g4, j + 1, v, 2, 512)
    cb4 = beside(bs4, bl4, 4)
    for c in cb4:
        c.start()
    own[1] = gathered_loss(cl, lrow, ROWS)
    cl = spread_loss(own.at[1], lz, zi, z_peer, NZ, 8)
    for c in cb4:
        c.wait()
    for row, v in zip((0, 3), landed(bl4)):
        put_back(g4, row, v, 2, 512)
    gin = jnp.zeros((64, 256), F32)
    for ky in range(3):
        rows = g4[2 - ky : 4 - ky].reshape(64, 1536)
        for kx in range(3):
            n = (ky * 3 + kx) * 256
            gin = gin + dot_t(rows[:, kx * 512 : (kx + 1) * 512], w4s[n : n + 256, :])

    for k in range(2):
        wide = spread_cols(gin[k * 32 : (k + 1) * 32], 2)
        for j in (2 * k, 2 * k + 1):
            v = rounded(a3[j] + s3[j] * wide)
            put_back(g3, j + 1, v, 4, 256)
            if j == 0:
                bs3[0] = v.astype(BF)
            if j == 3:
                bs3[1] = v.astype(BF)
    cb3 = beside(bs3, bl3, 5)
    for c in cb3:
        c.start()

    def back3(slab):
        out = 0.0
        for ky in range(3):
            rows = slab(ky)
            for kx in range(3):
                n = (ky * 3 + kx) * 128
                out = out + dot_t(rows[:, kx * 256 : (kx + 1) * 256], w3s[n : n + 128, :])
        return out

    def to2(row, g, side):
        wide = spread_cols(g, 4)
        for j in range(2):
            v = rounded(a2[2 * row + j] + s2[2 * row + j] * wide)
            put_back(g2, 2 * row + j + 1, v, 8, 128)
            if side == j:
                bs2[side] = v.astype(BF)

    gin = back3(lambda ky: g3[3 - ky : 5 - ky].reshape(128, 768))
    to2(1, gin[0:64], None)
    to2(2, gin[64:128], None)
    own[2] = gathered_loss(cl, lz, NZ)
    cl = spread_loss(own.at[2], ly, yi, y_peer, NY, 16)
    for c in cb3:
        c.wait()
    for row, v in zip((0, 5), landed(bl3)):
        put_back(g3, row, v, 4, 256)
    gin = back3(lambda ky: jnp.concatenate([g3[2 - ky], g3[5 - ky]], axis=0))
    to2(0, gin[0:64], 0)
    to2(3, gin[64:128], 1)
    cb2 = beside(bs2, bl2, 6)
    for c in cb2:
        c.start()

    def back2(row, side):
        g = 0.0
        for ky in range(3):
            g = g + dot_t(g2[row + 2 - ky], w2t[ky])
        for j in range(2):
            v = (a1[2 * row + j] + s1[2 * row + j] * g).astype(BF)
            gp1[2 * row + j + 1] = v
            if side == j:
                bs1[side] = v

    def inner_back2(row, carry):
        back2(row, None)
        return carry

    lax.fori_loop(1, 7, inner_back2, 0)
    for c in cb2:
        c.wait()
    for row, v in zip((0, 9), landed(bl2)):
        put_back(g2, row, v, 8, 128)
    back2(0, 0)
    back2(7, 1)
    cb1 = beside(bs1, bl1, 7)
    for c in cb1:
        c.start()

    g = jnp.zeros((128, 256), F32)
    for rr in range(1, 17):
        g = g + dot_t(gp1[rr], wb[rr])
    total = gathered_loss(cl, ly, NY)
    sums = jnp.sum(total, axis=1, keepdims=True)
    lanes = iota((8, 128), 1)
    counts = [32.0 * (128 >> s) * (256 >> s) for s in range(5)]
    scale = jnp.zeros((8, 128), F32)
    for s in range(5):
        scale = scale + jnp.where((lanes == s) & (rows_of == s), 1.0 / counts[s], 0.0)
    loss_ref[...] = jnp.sum(sums * scale, axis=0, keepdims=True)[:, 0:5]
    for c in cb1:
        c.wait()
    for rr, v in zip((0, 17), landed(bl1)):
        g = g + dot_t(v.astype(BF), wb[rr])
    across = jnp.transpose(g)
    lined = jnp.concatenate([across[d * 64 : (d + 1) * 64] for d in range(4)], axis=1)
    back = jnp.concatenate([onehot(col == base + d - 1) for d in range(4)], axis=0)
    high = lined.astype(BF)
    low = (lined - high.astype(F32)).astype(BF)
    out = dot(high, back) + dot(low, back)
    grad_ref[0] = out[0:48].reshape(3, 16, 256)


def on_device(*args):
    (real, fake, w1, w2, w3, w4, w5, *vectors) = args
    flat = [w.reshape(-1, w.shape[-1]) for w in (w2, w3, w4, w5)]
    vectors = [v.reshape(1, -1) for v in vectors]
    vmem = pl.BlockSpec(memory_space=pltpu.VMEM)
    anywhere = pl.BlockSpec(memory_space=pl.ANY)
    v = pltpu.VMEM
    dma = pltpu.SemaphoreType.DMA
    scratch = [
        v((3, 256, 128), BF), v((3, 128, 384), BF), v((1152, 256), BF), v((2304, 512), BF),
        v((4608, 512), BF), v((16, 512), F32), v((18, 256, 128), BF), v((8, 128), F32),
        v((2, 128, 256), BF),
        v((2, 10, 128, 256), BF), v((2, 6, 64, 384), BF), v((2, 4, 32, 768), BF),
        v((2, 10, 16, 1536), BF),
        v((10, 128, 384), BF), v((6, 64, 768), BF), v((4, 32, 1536), BF), v((10, 16, 1536), BF),
        v((18, 128, 128), BF),
        v((16, 128, 128), F32), v((16, 128, 128), F32), v((8, 128, 128), F32),
        v((8, 128, 128), F32), v((4, 64, 256), F32), v((4, 64, 256), F32),
        v((2, 32, 512), F32), v((2, 32, 512), F32),
        v((2, 16, 256), BF), v((2, 16, 256), BF), v((2, 128, 128), BF), v((2, 128, 128), BF),
        v((2, 64, 256), BF), v((2, 64, 256), BF), v((2, 32, 512), BF), v((2, 32, 512), BF),
        v((8, 16, 1024), BF), v((16, 1024), BF),
        v((2, 32, 512), BF), v((2, 32, 512), BF), v((2, 64, 256), BF), v((2, 64, 256), BF),
        v((2, 128, 128), BF), v((2, 128, 128), BF), v((2, 128, 128), BF), v((2, 128, 128), BF),
        v((5, 8, 128), F32), v((3, 8, 128), F32), v((8, 8, 128), F32), v((8, 8, 128), F32),
        v((4, 8, 128), F32),
        dma((6,)), dma((8, 2)), dma((8, 2)), dma((7,)), dma((7,)), dma((24,)), dma((24,)),
    ]
    losses, grads = pl.pallas_call(
        body,
        out_shape=(
            jax.ShapeDtypeStruct((1, 5), F32),
            jax.ShapeDtypeStruct((1, 3, 16, 256), F32),
        ),
        in_specs=[vmem] * 3 + [anywhere] * 4 + [vmem] * 10,
        out_specs=(vmem, vmem),
        scratch_shapes=scratch,
        compiler_params=pltpu.CompilerParams(
            collective_id=0, has_side_effects=True, vmem_limit_bytes=56 << 20
        ),
        name="whole_step",
    )(real, fake, w1, *flat, *vectors)
    return (losses.reshape(5), grads)


def solution(mesh):
    frames = P("dp", None, "rows", None)
    return jax.shard_map(
        on_device,
        mesh=mesh,
        in_specs=(frames, frames) + (P(),) * 15,
        out_specs=(P(), frames),
        check_vma=False,
    )
```

profile of v0, /device:TPU:1, one launch (start us, length us, event | category | flops | bytes accessed | tf_op | source)
XLA Modules:
  0.0 54.2 jit_solution(6145163197548921345)
XLA Ops:
  0.6 50.9 %whole_step.1 = (f32[1,5]{1,0:T(1,128)}, f32[1,3,16,256]{3,2,1,0:T(8,128)}) custom-call(bf16[1,3,16,256]{3,2,1,0:T(8,128)(2,1)} %real_ref.1, bf16[1,3,16,256]{3,2,1,0:T(8,128)(2,1)} %fake_ref.1, bf16[3,3,3,64]{3,2,1,0:T(4,128)(2,1)} %w1_ref.1, bf16[576,128]{1,0:T(8,128)(2,1)} %bitcast.18, bf16[1152,256]{1,0:T(8,128)(2,1)} %bitcast.17, ...), custom_call_target="tpu_custom_call" | custom-call | tf_op jit(solution)/shard_map/whole_step/pallas_call | solution.py:607
  51.6 1.1 %copy.21 = f32[5]{0:T(128)} copy(f32[5]{0:T(128)} %bitcast.29) | data formatting | bytes 40
  52.7 1.4 %copy.22 = f32[1,3,16,256]{3,2,1,0:T(8,128)} copy(f32[1,3,16,256]{3,2,1,0:T(8,128)} %get-tuple-element.9) | data formatting | bytes 98304
where the time goes:
time: 55.2 us; the launch traced here: 54.2 us
  Pallas kernels  50.9 us (92%)
  local copies, waits for them, and re-layouts  2.57 us (5%)
  between operations  0.65 us (1%)
    pallas_call x1, Pallas kernels, on_device(): pl.pallas_call(body, out_shape=(jax.ShapeDtypeStruct((1, 5), F32), jax.Sh...  50.9 us
    unnamed x2, local copies, waits for them, and re-layouts  2.57 us

commit v1 on v0

v1 whole, which is shorter than its diff:
```python
import functools

import jax
import jax.numpy as jnp
from jax import lax
from jax.experimental import pallas as pl
from jax.experimental.pallas import tpu as pltpu
from jax.sharding import PartitionSpec as P

MESH = pl.DeviceIdType.MESH
F32 = jnp.float32
BF = jnp.bfloat16
EPS = 1e-06
ROOT = 0.7978845608028654
CUBE = 0.044715

ROWS = 8
NZ = 8
NY = 4


def dot(a, b):
    return lax.dot_general(a, b, (((1,), (0,)), ((), ())), preferred_element_type=F32)


def dot_t(a, b):
    return lax.dot_general(a, b, (((1,), (1,)), ((), ())), preferred_element_type=F32)


def iota(shape, dim):
    return lax.broadcasted_iota(jnp.int32, shape, dim)


def onehot(cond):
    return jnp.where(cond, 1.0, 0.0).astype(BF)


def rounded(x):
    return x.astype(BF).astype(F32)


def gelu(x):
    t = jnp.tanh(x * (ROOT + (ROOT * CUBE) * (x * x)))
    return x * (0.5 + 0.5 * t)


def gelu_both(x):
    x2 = x * x
    t = jnp.tanh(x * (ROOT + (ROOT * CUBE) * x2))
    h = 0.5 + 0.5 * t
    slope = h + (0.5 * x) * (1.0 - t * t) * (ROOT + (3.0 * ROOT * CUBE) * x2)
    return x * h, slope


def tap(r, f, lin, total):
    a = lax.rsqrt(total(r * r) + EPS)
    b = lax.rsqrt(total(f * f) + EPS)
    nf = f * b
    d = r * a - nf
    ld = lin * d
    grad = (ld - nf * total(nf * ld)) * (-2.0 * b)
    return ld * d, grad


def lane_sum(x):
    return jnp.sum(x, axis=-1, keepdims=True)


def fold(x):
    m, c = x.shape
    y = jnp.sum(x.reshape(m // 8, 8, c), axis=0)
    out = y[:, 0:128]
    for j in range(1, c // 128):
        out = out + y[:, j * 128 : (j + 1) * 128]
    return out


def shifted(v, phases):
    c = v.shape[-1]
    q = iota((16, c), 0)
    n = phases * 16
    tail = jnp.where(q < 15, pltpu.roll(v[0:16], 15, 0), 0.0)
    head = jnp.where(q > 0, pltpu.roll(v[n - 16 : n], 1, 0), 0.0)
    if phases == 1:
        return head, tail
    left = jnp.concatenate([head, v[0 : n - 16]], axis=0)
    right = jnp.concatenate([v[16:n], tail], axis=0)
    return left, right


def pool_cols(v, phases):
    c = v.shape[-1]
    return jnp.sum(v.reshape(phases // 2, 2, 16, c), axis=1).reshape(phases * 8, c)


def spread_cols(v, phases):
    c = v.shape[-1]
    y = jnp.broadcast_to(v.reshape(phases, 1, 16, c), (phases, 2, 16, c))
    return y.reshape(phases * 32, c)


def body(
    real_ref, fake_ref, w1_ref, w2_hbm, w3_hbm, w4_hbm, w5_hbm,
    b1_ref, b2_ref, b3_ref, b4_ref, b5_ref, l1_ref, l2_ref, l3_ref, l4_ref, l5_ref,
    loss_ref, grad_ref,
    w2s, w2t, w3s, w4s, w5s, wsm, wb, vec, tt,
    x2, x3, x4, x5, g2, g3, g4, g5, gp1,
    act1, sl1, act2, sl2, act3, sl3,
    a1, s1, a2, s2, a3, s3, a4, s4,
    stage0, land0, stage5, land5, stage4, land4,
    parts, own, lrow, lz, ly,
    wsem, ssem, rsem, gsend, grecv, lsend, lrecv,
):
    dp = lax.axis_index("dp")
    me = lax.axis_index("rows")
    zi = lax.rem(dp, NZ)
    yi = lax.div(dp, NZ)
    not_first = me > 0
    not_last = me < ROWS - 1

    def row_peer(k):
        return (dp, lax.rem(me + k, ROWS))

    def z_peer(k):
        return (yi * NZ + lax.rem(zi + k, NZ), me)

    def y_peer(k):
        return (lax.rem(yi + k, NY) * NZ + zi, me)

    cw2 = [
        pltpu.make_async_copy(
            w2_hbm.at[pl.ds(ky * 192, 192)], w2s.at[ky, pl.ds(0, 192)], wsem.at[ky]
        )
        for ky in range(3)
    ]
    cw3 = pltpu.make_async_copy(w3_hbm, w3s, wsem.at[3])
    cw4 = pltpu.make_async_copy(w4_hbm, w4s, wsem.at[4])
    cw5 = pltpu.make_async_copy(w5_hbm, w5s, wsem.at[5])
    for c in cw2 + [cw3, cw4, cw5]:
        c.start()

    barrier = pltpu.get_barrier_semaphore()
    peers = (
        [row_peer(k) for k in range(1, ROWS)]
        + [z_peer(k) for k in range(1, NZ)]
        + [y_peer(k) for k in range(1, NY)]
    )
    for peer in peers:
        pl.semaphore_signal(barrier, inc=1, device_id=peer, device_id_type=MESH)

    def beside(first, second, land, n):
        up = pltpu.make_async_remote_copy(
            src_ref=first, dst_ref=land.at[1], send_sem=ssem.at[n, 0],
            recv_sem=rsem.at[n, 1], device_id=row_peer(ROWS - 1), device_id_type=MESH,
        )
        down = pltpu.make_async_remote_copy(
            src_ref=second, dst_ref=land.at[0], send_sem=ssem.at[n, 1],
            recv_sem=rsem.at[n, 0], device_id=row_peer(1), device_id_type=MESH,
        )
        return up, down

    stage0[0:48] = real_ref[0].reshape(48, 256)
    stage0[48:96] = fake_ref[0].reshape(48, 256)

    wsm[...] = jnp.zeros_like(wsm)
    for ky in range(3):
        for kx in range(3):
            piece = w1_ref[ky, kx].astype(F32)
            for p in range(2):
                lane = (kx + p) * 128 + p * 64
                wsm[ky * 3 : ky * 3 + 3, lane : lane + 64] = piece
    small = wsm[...].astype(BF)

    def band(k, carry):
        idx = iota((64, 16), 0)
        n = iota((64, 16), 1)
        ky = jnp.where(n >= 3, 1, 0) + jnp.where(n >= 6, 1, 0)
        ci = n - 3 * ky
        for half in range(2):
            row = jnp.where(k < 8, 2 * k + half, 17 * half - 1)
            at = row + ky - 1
            inner = (idx >> 4 == ci) & ((idx & 15) == at) & (idx < 48)
            above = (idx - 48 == ci) & (at == -1)
            below = (idx - 51 == ci) & (at == 16)
            block = dot(onehot((inner | above | below) & (n < 9)), small).astype(BF)
            for d in range(4):
                wb[k, d * 64 : (d + 1) * 64, half * 128 : (half + 1) * 128] = block[
                    :, d * 128 : (d + 1) * 128
                ]
        return carry

    lax.fori_loop(0, 9, band, 0)

    for row, ref in ((0, b1_ref), (1, l1_ref)):
        for q in range(4):
            vec[row : row + 1, q * 64 : (q + 1) * 64] = ref[...]
    ones_part = onehot(iota((256, 256), 0) >> 6 == iota((256, 256), 1) >> 6)
    ones_full = jnp.full((128, 128), 1.0, BF)

    def sum_part(x):
        return dot(x.astype(BF), ones_part)

    def sum_full(x):
        return dot(x.astype(BF), ones_full)

    parts[...] = jnp.zeros_like(parts)
    w2s[:, 192:256, :] = jnp.zeros((3, 64, 128), BF)

    pos = iota((128, 256), 0)
    col = iota((128, 256), 1)
    base = 16 * (pos & 15) + 2 * (pos >> 4)
    take = onehot(col == base)

    def patches(slot, images, sources):
        for i in range(2):
            halo = jnp.zeros((16, 256), F32)
            for source, row, off, ok in sources:
                j = iota((16, 96), 0) - off
                k = iota((16, 96), 1)
                pick = (j >= 0) & (j < 3) & (k == i * 48 + j * 16 + row)
                if ok is not None:
                    pick = pick & ok
                halo = halo + dot(onehot(pick), source)
            whole = jnp.concatenate([images[i * 48 : (i + 1) * 48].astype(F32), halo], axis=0)
            cols = iota((64, 256), 1)
            turned = []
            for d in range(4):
                dx = d - 1
                moved = whole if dx == 0 else pltpu.roll(whole, (-dx) % 256, 1)
                moved = jnp.where((cols + dx >= 0) & (cols + dx < 256), moved, 0.0)
                turned.append(moved.astype(BF))
            tt[slot, i * 128 : (i + 1) * 128, :] = dot_t(
                take, jnp.concatenate(turned, axis=0)
            ).astype(BF)

    mine = stage0[...]
    patches(0, mine, ())

    pl.semaphore_wait(barrier, len(peers))
    c0 = beside(stage0, stage0, land0, 0)
    for c in c0:
        c.start()

    lane = iota((128, 128), 1)
    bias1 = vec[0:1, :]
    lin1 = vec[1:2, :]

    def put2(row, v):
        for i in range(2):
            w = v[i * 128 : (i + 1) * 128]
            left, right = shifted(w, 8)
            x2[row, i * 128 : (i + 1) * 128, 0:128] = jnp.where(lane < 64, left, w).astype(BF)
            x2[row, i * 128 : (i + 1) * 128, 128:256] = right.astype(BF)

    def segment1(slot, k, p, keep, ok):
        pre = dot(tt[slot], wb[k]) + bias1
        if keep is None:
            act = rounded(gelu(pre))
        else:
            act_f, slope = gelu_both(pre[128:256])
            act = rounded(jnp.concatenate([gelu(pre[0:128]), act_f], axis=0))
            if keep == "left":
                act1[8, :, 0:128] = act[:, 128:256].astype(BF)
                sl1[8, :, 0:128] = slope[:, 128:256]
            elif keep == "right":
                act1[8, :, 128:256] = act[:, 0:128].astype(BF)
                sl1[8, :, 128:256] = slope[:, 0:128]
            else:
                act1[k] = act.astype(BF)
                sl1[k] = slope
        s = act[:, 0:128] + act[:, 128:256]
        v = rounded((s + pltpu.roll(s, 64, 1)) * 0.25)
        if ok is not None:
            v = jnp.where(ok, v, 0.0)
        put2(p, v)

    def tap1(k, counted):
        act = act1[k].astype(F32)
        terms, grad = tap(act[0:128], act[128:256], lin1, sum_part)
        if counted:
            parts[0] += fold(terms)
        slope = sl1[k]
        a1[k] = slope * grad
        s1[k] = slope * 0.25

    def inner1(n, carry):
        for j in range(2):
            k = 1 + 2 * n + j
            segment1(0, k, 7 + k, "own", None)
        return carry

    lax.fori_loop(0, 3, inner1, 0)

    def inner_tap1(n, carry):
        for j in range(2):
            tap1(1 + 2 * n + j, True)
        return carry

    lax.fori_loop(0, 3, inner_tap1, 0)

    for c in cw2:
        c.wait()
    for ky in range(3):
        for kx in range(3):
            piece = w2s[ky, kx * 64 : (kx + 1) * 64, :]
            w2t[ky, 0:64, kx * 128 : (kx + 1) * 128] = piece
            w2t[ky, 64:128, kx * 128 : (kx + 1) * 128] = piece

    for c in c0:
        c.wait()
    upper = land0[0]
    lower = land0[1]
    patches(1, mine, ((upper, 15, 0, not_first), (lower, 0, 3, not_last)))
    patches(2, upper, ((mine, 0, 3, None),))
    patches(3, lower, ((mine, 15, 0, None),))
    segment1(2, 7, 6, "left", not_first)
    segment1(1, 0, 7, "own", None)
    segment1(1, 7, 14, "own", None)
    segment1(3, 0, 15, "right", not_last)

    def outer1(n, carry):
        for j in range(2):
            k = 1 + 2 * n + j
            segment1(2, k, k - 1, None, not_first)
            segment1(3, k, 15 + k, None, not_last)
        return carry

    lax.fori_loop(0, 3, outer1, 0)

    def put(ref, row, v, phases, c):
        n = phases * 16
        for i in range(2):
            w = v[i * n : (i + 1) * n]
            left, right = shifted(w, phases)
            ref[row, i * n : (i + 1) * n, 0:c] = left.astype(BF)
            ref[row, i * n : (i + 1) * n, c : 2 * c] = w.astype(BF)
            ref[row, i * n : (i + 1) * n, 2 * c : 3 * c] = right.astype(BF)

    def both(pre, n):
        parts_of = []
        slopes = []
        for row in range(2):
            top = 2 * row * n
            parts_of.append(gelu(pre[top : top + n]))
            act, slope = gelu_both(pre[top + n : top + 2 * n])
            parts_of.append(act)
            slopes.append(slope)
        return rounded(jnp.concatenate(parts_of, axis=0)), jnp.concatenate(slopes, axis=0)

    def segment2(m):
        pre = b2_ref[...]
        for ky in range(3):
            rows = x2[pl.ds(2 * m + ky, 2)].reshape(512, 256)
            pre = pre + dot(rows, w2s[ky])
        act, slope = both(pre, 128)
        act2[m] = act.astype(BF)
        sl2[m] = slope
        v = rounded(pool_cols(act[0:256] + act[256:512], 16) * 0.25)
        ok = ((m >= 3) | not_first) & ((m < 7) | not_last)
        put(x3, m, jnp.where(ok, v, 0.0), 4, 128)

    def loop2(n, carry):
        for j in range(2):
            segment2(2 * n + j)
        return carry

    lax.fori_loop(0, 5, loop2, 0)

    cw3.wait()

    def segment3(n):
        pre = b3_ref[...]
        for ky in range(3):
            rows = x3[pl.ds(2 * n + ky, 2)].reshape(256, 384)
            pre = pre + dot(rows, w3s[ky * 384 : (ky + 1) * 384, :])
        act, slope = both(pre, 64)
        act3[n] = act.astype(BF)
        sl3[n] = slope
        v = rounded(pool_cols(act[0:128] + act[128:256], 8) * 0.25)
        ok = ((n >= 1) | not_first) & ((n < 3) | not_last)
        put(x4, n, jnp.where(ok, v, 0.0), 2, 256)

    def loop3(n, carry):
        for j in range(2):
            segment3(2 * n + j)
        return carry

    lax.fori_loop(0, 2, loop3, 0)

    cw4.wait()
    pre = b4_ref[...]
    for ky in range(3):
        rows = x4[ky : ky + 2].reshape(128, 768)
        pre = pre + dot(rows, w4s[ky * 768 : (ky + 1) * 768, :])
    act, slope = both(pre, 32)
    stage5[...] = (pool_cols(act[0:64] + act[64:128], 4) * 0.25).astype(BF)
    c5 = [
        pltpu.make_async_remote_copy(
            src_ref=stage5, dst_ref=land5.at[me], send_sem=gsend.at[k - 1],
            recv_sem=grecv.at[k - 1], device_id=row_peer(k), device_id_type=MESH,
        )
        for k in range(1, ROWS)
    ]
    for c in c5:
        c.start()
    land5[me] = stage5[...]

    act = act.reshape(2, 2, 32, 512)
    terms, grad = tap(
        act[:, 0].reshape(64, 512), act[:, 1].reshape(64, 512), l4_ref[...], lane_sum
    )
    parts[3] += fold(terms)
    a = slope * (64.0 * grad)
    s = slope * 0.25
    a4[...] = a.reshape(2, 32, 512)
    s4[...] = s.reshape(2, 32, 512)
    stage4[0:2] = a.astype(BF).reshape(2, 32, 512)
    stage4[2:4] = s.astype(BF).reshape(2, 32, 512)
    c4 = beside(stage4, stage4, land4, 1)
    for c in c4:
        c.start()

    def tap3(n, counted):
        act = act3[n].astype(F32).reshape(2, 2, 64, 256)
        slope = sl3[n]
        terms, grad = tap(
            act[:, 0].reshape(128, 256), act[:, 1].reshape(128, 256), l3_ref[...], lane_sum
        )
        if counted:
            parts[2] += fold(terms)
        a3[2 * n : 2 * n + 2] = (slope * (16.0 * grad)).reshape(2, 64, 256)
        s3[2 * n : 2 * n + 2] = (slope * 0.25).reshape(2, 64, 256)

    def tap2(m, counted):
        act = act2[m].astype(F32).reshape(2, 2, 128, 128)
        slope = sl2[m]
        terms, grad = tap(
            act[:, 0].reshape(256, 128), act[:, 1].reshape(256, 128), l2_ref[...], sum_full
        )
        if counted:
            parts[1] += fold(terms)
        a2[pl.ds(2 * m - 4, 2)] = (slope * (4.0 * grad)).reshape(2, 128, 128)
        s2[pl.ds(2 * m - 4, 2)] = (slope * 0.25).reshape(2, 128, 128)

    tap1(0, True)
    tap1(7, True)
    tap1(8, False)
    tap3(1, True)
    tap3(2, True)

    def loop_tap2(n, carry):
        for j in range(2):
            tap2(3 + 2 * n + j, True)
        return carry

    lax.fori_loop(0, 2, loop_tap2, 0)

    def spread_loss(src, land, slot, peer, count, first):
        copies = [
            pltpu.make_async_remote_copy(
                src_ref=src, dst_ref=land.at[slot], send_sem=lsend.at[first + k],
                recv_sem=lrecv.at[first + k], device_id=peer(k), device_id_type=MESH,
            )
            for k in range(1, count)
        ]
        for c in copies:
            c.start()
        land[slot] = src[...]
        return copies

    def gathered_loss(copies, land, count):
        for c in copies:
            c.wait()
        total = land[0]
        for j in range(1, count):
            total = total + land[j]
        return total

    rows_of = iota((8, 128), 0)
    sums = jnp.zeros((8, 128), F32)
    for s in range(4):
        sums = sums + jnp.where(rows_of == s, jnp.sum(parts[s], axis=0, keepdims=True), 0.0)
    own[0] = sums
    cl = spread_loss(own.at[0], lrow, me, row_peer, ROWS, 0)

    tap2(2, False)
    tap2(7, False)
    tap3(0, False)
    tap3(3, False)

    for row in (0, 9):
        x5[row] = jnp.zeros((32, 1536), BF)
    for row in (0, 1, 10, 11):
        g5[row] = jnp.zeros((16, 1536), BF)
    cw5.wait()
    for c in c5:
        c.wait()
    for row in range(ROWS):
        put(x5, row + 1, land5[row].astype(F32), 1, 512)
    pre = b5_ref[...]
    for ky in range(3):
        rows = x5[ky : ky + 8].reshape(256, 1536)
        pre = pre + dot(rows, w5s[ky * 1536 : (ky + 1) * 1536, :])
    pre = pre.reshape(8, 2, 16, 512)
    act_r = rounded(gelu(pre[:, 0].reshape(128, 512)))
    act_f, slope = gelu_both(pre[:, 1].reshape(128, 512))
    act_f = rounded(act_f)
    terms, grad = tap(act_r, act_f, l5_ref[...], lane_sum)
    gpre = rounded(slope * (256.0 * grad))

    def put_back(ref, row, v, phases, c):
        left, right = shifted(v, phases)
        ref[row, :, 0:c] = right.astype(BF)
        ref[row, :, c : 2 * c] = v.astype(BF)
        ref[row, :, 2 * c : 3 * c] = left.astype(BF)

    for row in range(ROWS):
        put_back(g5, row + 2, gpre[row * 16 : (row + 1) * 16], 1, 512)
    fifth = jnp.sum(fold(terms), axis=0, keepdims=True)
    own[1] = gathered_loss(cl, lrow, ROWS) + jnp.where(rows_of == 4, fifth, 0.0)
    cl = spread_loss(own.at[1], lz, zi, z_peer, NZ, 8)

    gin = jnp.zeros((48, 512), F32)
    for ky in range(3):
        rows = g5[pl.ds(me + 2 - ky, 3)].reshape(48, 1536)
        for kx in range(3):
            n = (ky * 3 + kx) * 512
            gin = gin + dot_t(rows[:, kx * 512 : (kx + 1) * 512], w5s[n : n + 512, :])

    for c in c4:
        c.wait()
    for u in range(6):
        wide = spread_cols(gin[(u // 2) * 16 : (u // 2 + 1) * 16], 1)
        if 2 <= u < 4:
            v = a4[u - 2] + s4[u - 2] * wide
        else:
            side, j, ok = (0, u, not_first) if u < 2 else (1, u - 4, not_last)
            a = land4[side, j].astype(F32)
            s = land4[side, 2 + j].astype(F32)
            v = jnp.where(ok, a + s * wide, 0.0)
        put_back(g4, u, rounded(v), 2, 512)
    gin = jnp.zeros((128, 256), F32)
    for ky in range(3):
        rows = g4[2 - ky : 6 - ky].reshape(128, 1536)
        for kx in range(3):
            n = (ky * 3 + kx) * 256
            gin = gin + dot_t(rows[:, kx * 512 : (kx + 1) * 512], w4s[n : n + 256, :])

    for j in range(8):
        wide = spread_cols(gin[(j // 2) * 32 : (j // 2 + 1) * 32], 2)
        v = a3[j] + s3[j] * wide
        if j < 2:
            v = jnp.where(not_first, v, 0.0)
        if j >= 6:
            v = jnp.where(not_last, v, 0.0)
        put_back(g3, j, rounded(v), 4, 256)
    gin = 0.0
    for ky in range(3):
        rows = g3[2 - ky : 8 - ky].reshape(384, 768)
        for kx in range(3):
            n = (ky * 3 + kx) * 128
            gin = gin + dot_t(rows[:, kx * 256 : (kx + 1) * 256], w3s[n : n + 128, :])
    own[2] = gathered_loss(cl, lz, NZ)
    cl = spread_loss(own.at[2], ly, yi, y_peer, NY, 16)

    for j in range(12):
        wide = spread_cols(gin[(j // 2) * 64 : (j // 2 + 1) * 64], 4)
        v = a2[j] + s2[j] * wide
        if j < 2:
            v = jnp.where(not_first, v, 0.0)
        if j >= 10:
            v = jnp.where(not_last, v, 0.0)
        put_back(g2, j, rounded(v), 8, 128)

    def inner_back2(n, carry):
        g = 0.0
        for ky in range(3):
            rows = g2[pl.ds(2 * n + 3 - ky, 2)].reshape(256, 384)
            g = g + dot_t(rows, w2t[ky])
        for j in range(2):
            k = 2 * n + j
            one = g[j * 128 : (j + 1) * 128]
            wide = jnp.concatenate([one, one], axis=1)
            gp1[k] = (a1[k] + s1[k] * wide).astype(BF)
        return carry

    lax.fori_loop(0, 4, inner_back2, 0)
    g = 0.0
    for ky in range(3):
        rows = jnp.concatenate([g2[2 - ky], g2[11 - ky]], axis=0)
        g = g + dot_t(rows, w2t[ky])
    above = jnp.where(not_first, a1[8, :, 0:128] + s1[8, :, 0:128] * g[0:128], 0.0)
    below = jnp.where(not_last, a1[8, :, 128:256] + s1[8, :, 128:256] * g[128:256], 0.0)
    gp1[8] = jnp.concatenate([above, below], axis=1).astype(BF)

    g = jnp.zeros((128, 256), F32)
    for k in range(9):
        g = g + dot_t(gp1[k], wb[k])
    across = jnp.transpose(g)
    lined = jnp.concatenate([across[d * 64 : (d + 1) * 64] for d in range(4)], axis=1)
    back = jnp.concatenate([onehot(col == base + d - 1) for d in range(4)], axis=0)
    high = lined.astype(BF)
    low = (lined - high.astype(F32)).astype(BF)
    out = dot(high, back) + dot(low, back)
    grad_ref[0] = out[0:48].reshape(3, 16, 256)

    total = gathered_loss(cl, ly, NY)
    sums = jnp.sum(total, axis=1, keepdims=True)
    lanes = iota((8, 128), 1)
    counts = [32.0 * (128 >> s) * (256 >> s) for s in range(5)]
    scale = jnp.zeros((8, 128), F32)
    for s in range(5):
        scale = scale + jnp.where((lanes == s) & (rows_of == s), 1.0 / counts[s], 0.0)
    loss_ref[...] = jnp.sum(sums * scale, axis=0, keepdims=True)[:, 0:5]


def on_device(*args):
    (real, fake, w1, w2, w3, w4, w5, *vectors) = args
    flat = [w.reshape(-1, w.shape[-1]) for w in (w2, w3, w4, w5)]
    vectors = [v.reshape(1, -1) for v in vectors]
    vmem = pl.BlockSpec(memory_space=pltpu.VMEM)
    anywhere = pl.BlockSpec(memory_space=pl.ANY)
    v = pltpu.VMEM
    dma = pltpu.SemaphoreType.DMA
    scratch = [
        v((3, 256, 128), BF), v((3, 128, 384), BF), v((1152, 256), BF), v((2304, 512), BF),
        v((4608, 512), BF), v((16, 512), F32), v((9, 256, 256), BF), v((8, 256), F32),
        v((4, 256, 256), BF),
        v((22, 256, 256), BF), v((10, 128, 384), BF), v((4, 64, 768), BF), v((10, 32, 1536), BF),
        v((12, 128, 384), BF), v((8, 64, 768), BF), v((6, 32, 1536), BF), v((12, 16, 1536), BF),
        v((9, 128, 256), BF),
        v((9, 256, 256), BF), v((9, 128, 256), F32), v((10, 512, 128), BF),
        v((10, 256, 128), F32), v((4, 256, 256), BF), v((4, 128, 256), F32),
        v((9, 128, 256), F32), v((9, 128, 256), F32), v((12, 128, 128), F32),
        v((12, 128, 128), F32), v((8, 64, 256), F32), v((8, 64, 256), F32),
        v((2, 32, 512), F32), v((2, 32, 512), F32),
        v((96, 256), BF), v((2, 96, 256), BF), v((32, 512), BF), v((8, 32, 512), BF),
        v((4, 32, 512), BF), v((2, 4, 32, 512), BF),
        v((5, 8, 128), F32), v((3, 8, 128), F32), v((8, 8, 128), F32), v((8, 8, 128), F32),
        v((4, 8, 128), F32),
        dma((6,)), dma((2, 2)), dma((2, 2)), dma((7,)), dma((7,)), dma((24,)), dma((24,)),
    ]
    losses, grads = pl.pallas_call(
        body,
        out_shape=(
            jax.ShapeDtypeStruct((1, 5), F32),
            jax.ShapeDtypeStruct((1, 3, 16, 256), F32),
        ),
        in_specs=[vmem] * 3 + [anywhere] * 4 + [vmem] * 10,
        out_specs=(vmem, vmem),
        scratch_shapes=scratch,
        compiler_params=pltpu.CompilerParams(
            collective_id=0, has_side_effects=True, vmem_limit_bytes=56 << 20
        ),
        name="whole_step",
    )(real, fake, w1, *flat, *vectors)
    return (losses.reshape(5), grads)


def solution(mesh):
    frames = P("dp", None, "rows", None)
    return jax.shard_map(
        on_device,
        mesh=mesh,
        in_specs=(frames, frames) + (P(),) * 15,
        out_specs=(P(), frames),
        check_vma=False,
    )
```

time: 55.2 us -> 44 us (0.80); the launches traced: 54.2 us -> 43.8 us
  Pallas kernels: 50.9 us -> 40.6 us
    pallas_call x1, Pallas kernels: 50.9 us -> 40.6 us  [on_device(): pl.pallas_call(body, out_shape=(jax.ShapeDtypeStruct((1, 5), F32), jax.Sh...]
where the time goes in v1:
time: 44 us; the launch traced here: 43.8 us
  Pallas kernels  40.6 us (92%)
  local copies, waits for them, and re-layouts  2.57 us (6%)
  between operations  0.65 us (1%)
    pallas_call x1, Pallas kernels, on_device(): pl.pallas_call(body, out_shape=(jax.ShapeDtypeStruct((1, 5), F32), jax.Sh...  40.6 us
    unnamed x2, local copies, waits for them, and re-layouts  2.57 us

profile of v1, /device:TPU:1, one launch (start us, length us, event | category | flops | bytes accessed | tf_op | source)
XLA Modules:
  0.0 43.8 jit_solution(15894996242725385175)
XLA Ops:
  0.6 40.6 %whole_step.1 = (f32[1,5]{1,0:T(1,128)}, f32[1,3,16,256]{3,2,1,0:T(8,128)}) custom-call(bf16[1,3,16,256]{3,2,1,0:T(8,128)(2,1)} %real_ref.1, bf16[1,3,16,256]{3,2,1,0:T(8,128)(2,1)} %fake_ref.1, bf16[3,3,3,64]{3,2,1,0:T(4,128)(2,1)} %w1_ref.1, bf16[576,128]{1,0:T(8,128)(2,1)} %bitcast.18, bf16[1152,256]{1,0:T(8,128)(2,1)} %bitcast.17, ...), custom_call_target="tpu_custom_call" | custom-call | tf_op jit(solution)/shard_map/whole_step/pallas_call | solution.py:643
  41.3 1.1 %copy.21 = f32[5]{0:T(128)} copy(f32[5]{0:T(128)} %bitcast.29) | data formatting | bytes 40
  42.4 1.4 %copy.22 = f32[1,3,16,256]{3,2,1,0:T(8,128)} copy(f32[1,3,16,256]{3,2,1,0:T(8,128)} %get-tuple-element.9) | data formatting | bytes 98304

commit v2 on v1

--- a/solution.py
+++ b/solution.py
@@ -171,13 +171,13 @@
                 wsm[ky * 3 : ky * 3 + 3, lane : lane + 64] = piece
     small = wsm[...].astype(BF)
 
-    def band(k, carry):
+    for k in range(9):
         idx = iota((64, 16), 0)
         n = iota((64, 16), 1)
         ky = jnp.where(n >= 3, 1, 0) + jnp.where(n >= 6, 1, 0)
         ci = n - 3 * ky
         for half in range(2):
-            row = jnp.where(k < 8, 2 * k + half, 17 * half - 1)
+            row = 2 * k + half if k < 8 else 17 * half - 1
             at = row + ky - 1
             inner = (idx >> 4 == ci) & ((idx & 15) == at) & (idx < 48)
             above = (idx - 48 == ci) & (at == -1)
@@ -187,9 +187,6 @@
                 wb[k, d * 64 : (d + 1) * 64, half * 128 : (half + 1) * 128] = block[
                     :, d * 128 : (d + 1) * 128
                 ]
-        return carry
-
-    lax.fori_loop(0, 9, band, 0)
 
     for row, ref in ((0, b1_ref), (1, l1_ref)):
         for q in range(4):
@@ -283,20 +280,10 @@
         a1[k] = slope * grad
         s1[k] = slope * 0.25
 
-    def inner1(n, carry):
-        for j in range(2):
-            k = 1 + 2 * n + j
-            segment1(0, k, 7 + k, "own", None)
-        return carry
-
-    lax.fori_loop(0, 3, inner1, 0)
-
-    def inner_tap1(n, carry):
-        for j in range(2):
-            tap1(1 + 2 * n + j, True)
-        return carry
-
-    lax.fori_loop(0, 3, inner_tap1, 0)
+    for k in range(1, 7):
+        segment1(0, k, 7 + k, "own", None)
+    for k in range(1, 7):
+        tap1(k, True)
 
     for c in cw2:
         c.wait()
@@ -318,14 +305,9 @@
     segment1(1, 7, 14, "own", None)
     segment1(3, 0, 15, "right", not_last)
 
-    def outer1(n, carry):
-        for j in range(2):
-            k = 1 + 2 * n + j
-            segment1(2, k, k - 1, None, not_first)
-            segment1(3, k, 15 + k, None, not_last)
-        return carry
-
-    lax.fori_loop(0, 3, outer1, 0)
+    for k in range(1, 7):
+        segment1(2, k, k - 1, None, not_first)
+        segment1(3, k, 15 + k, None, not_last)
 
     def put(ref, row, v, phases, c):
         n = phases * 16
@@ -350,42 +332,43 @@
     def segment2(m):
         pre = b2_ref[...]
         for ky in range(3):
-            rows = x2[pl.ds(2 * m + ky, 2)].reshape(512, 256)
+            rows = x2[2 * m + ky : 2 * m + ky + 2].reshape(512, 256)
             pre = pre + dot(rows, w2s[ky])
-        act, slope = both(pre, 128)
-        act2[m] = act.astype(BF)
-        sl2[m] = slope
+        if 2 <= m < 8:
+            act, slope = both(pre, 128)
+            act2[m - 2] = act.astype(BF)
+            sl2[m - 2] = slope
+        else:
+            act = rounded(gelu(pre))
         v = rounded(pool_cols(act[0:256] + act[256:512], 16) * 0.25)
-        ok = ((m >= 3) | not_first) & ((m < 7) | not_last)
-        put(x3, m, jnp.where(ok, v, 0.0), 4, 128)
-
-    def loop2(n, carry):
-        for j in range(2):
-            segment2(2 * n + j)
-        return carry
-
-    lax.fori_loop(0, 5, loop2, 0)
+        if m < 3:
+            v = jnp.where(not_first, v, 0.0)
+        if m >= 7:
+            v = jnp.where(not_last, v, 0.0)
+        put(x3, m, v, 4, 128)
+
+    for m in range(10):
+        segment2(m)
 
     cw3.wait()
 
     def segment3(n):
         pre = b3_ref[...]
         for ky in range(3):
-            rows = x3[pl.ds(2 * n + ky, 2)].reshape(256, 384)
+            rows = x3[2 * n + ky : 2 * n + ky + 2].reshape(256, 384)
             pre = pre + dot(rows, w3s[ky * 384 : (ky + 1) * 384, :])
         act, slope = both(pre, 64)
         act3[n] = act.astype(BF)
         sl3[n] = slope
         v = rounded(pool_cols(act[0:128] + act[128:256], 8) * 0.25)
-        ok = ((n >= 1) | not_first) & ((n < 3) | not_last)
-        put(x4, n, jnp.where(ok, v, 0.0), 2, 256)
-
-    def loop3(n, carry):
-        for j in range(2):
-            segment3(2 * n + j)
-        return carry
-
-    lax.fori_loop(0, 2, loop3, 0)
+        if n < 1:
+            v = jnp.where(not_first, v, 0.0)
+        if n >= 3:
+            v = jnp.where(not_last, v, 0.0)
+        put(x4, n, v, 2, 256)
+
+    for n in range(4):
+        segment3(n)
 
     cw4.wait()
     pre = b4_ref[...]
@@ -432,15 +415,15 @@
         s3[2 * n : 2 * n + 2] = (slope * 0.25).reshape(2, 64, 256)
 
     def tap2(m, counted):
-        act = act2[m].astype(F32).reshape(2, 2, 128, 128)
-        slope = sl2[m]
+        act = act2[m - 2].astype(F32).reshape(2, 2, 128, 128)
+        slope = sl2[m - 2]
         terms, grad = tap(
             act[:, 0].reshape(256, 128), act[:, 1].reshape(256, 128), l2_ref[...], sum_full
         )
         if counted:
             parts[1] += fold(terms)
-        a2[pl.ds(2 * m - 4, 2)] = (slope * (4.0 * grad)).reshape(2, 128, 128)
-        s2[pl.ds(2 * m - 4, 2)] = (slope * 0.25).reshape(2, 128, 128)
+        a2[2 * m - 4 : 2 * m - 2] = (slope * (4.0 * grad)).reshape(2, 128, 128)
+        s2[2 * m - 4 : 2 * m - 2] = (slope * 0.25).reshape(2, 128, 128)
 
     tap1(0, True)
     tap1(7, True)
@@ -448,12 +431,8 @@
     tap3(1, True)
     tap3(2, True)
 
-    def loop_tap2(n, carry):
-        for j in range(2):
-            tap2(3 + 2 * n + j, True)
-        return carry
-
-    lax.fori_loop(0, 2, loop_tap2, 0)
+    for m in range(3, 7):
+        tap2(m, True)
 
     def spread_loss(src, land, slot, peer, count, first):
         copies = [
@@ -572,19 +551,16 @@
             v = jnp.where(not_last, v, 0.0)
         put_back(g2, j, rounded(v), 8, 128)
 
-    def inner_back2(n, carry):
+    for n in range(4):
         g = 0.0
         for ky in range(3):
-            rows = g2[pl.ds(2 * n + 3 - ky, 2)].reshape(256, 384)
+            rows = g2[2 * n + 3 - ky : 2 * n + 5 - ky].reshape(256, 384)
             g = g + dot_t(rows, w2t[ky])
         for j in range(2):
             k = 2 * n + j
             one = g[j * 128 : (j + 1) * 128]
             wide = jnp.concatenate([one, one], axis=1)
             gp1[k] = (a1[k] + s1[k] * wide).astype(BF)
-        return carry
-
-    lax.fori_loop(0, 4, inner_back2, 0)
     g = 0.0
     for ky in range(3):
         rows = jnp.concatenate([g2[2 - ky], g2[11 - ky]], axis=0)
@@ -612,6 +588,11 @@
     for s in range(5):
         scale = scale + jnp.where((lanes == s) & (rows_of == s), 1.0 / counts[s], 0.0)
     loss_ref[...] = jnp.sum(sums * scale, axis=0, keepdims=True)[:, 0:5]
+
+
+def hand_on(losses_ref, grads_ref, loss_ref, grad_ref):
+    loss_ref[...] = losses_ref[...]
+    grad_ref[...] = grads_ref[...]
 
 
 def on_device(*args):
@@ -629,8 +610,8 @@
         v((22, 256, 256), BF), v((10, 128, 384), BF), v((4, 64, 768), BF), v((10, 32, 1536), BF),
         v((12, 128, 384), BF), v((8, 64, 768), BF), v((6, 32, 1536), BF), v((12, 16, 1536), BF),
         v((9, 128, 256), BF),
-        v((9, 256, 256), BF), v((9, 128, 256), F32), v((10, 512, 128), BF),
-        v((10, 256, 128), F32), v((4, 256, 256), BF), v((4, 128, 256), F32),
+        v((9, 256, 256), BF), v((9, 128, 256), F32), v((6, 512, 128), BF),
+        v((6, 256, 128), F32), v((4, 256, 256), BF), v((4, 128, 256), F32),
         v((9, 128, 256), F32), v((9, 128, 256), F32), v((12, 128, 128), F32),
         v((12, 128, 128), F32), v((8, 64, 256), F32), v((8, 64, 256), F32),
         v((2, 32, 512), F32), v((2, 32, 512), F32),
@@ -654,6 +635,16 @@
         ),
         name="whole_step",
     )(real, fake, w1, *flat, *vectors)
+    losses, grads = pl.pallas_call(
+        hand_on,
+        out_shape=(
+            jax.ShapeDtypeStruct((1, 5), F32),
+            jax.ShapeDtypeStruct((1, 3, 16, 256), F32),
+        ),
+        in_specs=[vmem] * 2,
+        out_specs=(vmem, vmem),
+        name="hand_on",
+    )(losses, grads)
     return (losses.reshape(5), grads)
 
 

time: 44 us -> 39.3 us (0.89)
  local copies, waits for them, and re-layouts: 2.57 us -> 0 us
  Pallas kernels: 40.6 us -> 38.5 us
    pallas_call x1, Pallas kernels: 40.6 us -> 37 us  [on_device(): pl.pallas_call(body, out_shape=(jax.ShapeDtypeStruct((1, 5), F32), jax.Sh...]
    unnamed x2 -> x0, local copies, waits for them, and re-layouts: 2.57 us -> none
    pallas_call x0 -> x1, Pallas kernels: none -> 1.43 us  [on_device(): pl.pallas_call(hand_on, out_shape=(jax.ShapeDtypeStruct((1, 5), F32), jax...]
where the time goes in v2:
time: 39.3 us; the launch traced here: 39.1 us
  Pallas kernels  38.5 us (98%)
  between operations  0.65 us (2%)
    pallas_call x1, Pallas kernels, on_device(): pl.pallas_call(body, out_shape=(jax.ShapeDtypeStruct((1, 5), F32), jax.Sh...  37 us
    pallas_call x1, Pallas kernels, on_device(): pl.pallas_call(hand_on, out_shape=(jax.ShapeDtypeStruct((1, 5), F32), jax...  1.43 us

profile of v2, /device:TPU:1, one launch (start us, length us, event | category | flops | bytes accessed | tf_op | source)
XLA Modules:
  0.0 39.1 jit_solution(8451725325393644076)
XLA Ops:
  0.6 37.0 %whole_step.1 = (f32[1,5]{1,0:T(1,128)}, f32[1,3,16,256]{3,2,1,0:T(8,128)}) custom-call(bf16[1,3,16,256]{3,2,1,0:T(8,128)(2,1)} %real_ref.1, bf16[1,3,16,256]{3,2,1,0:T(8,128)(2,1)} %fake_ref.1, bf16[3,3,3,64]{3,2,1,0:T(4,128)(2,1)} %w1_ref.1, bf16[576,128]{1,0:T(8,128)(2,1)} %bitcast.18, bf16[1152,256]{1,0:T(8,128)(2,1)} %bitcast.17, ...), custom_call_target="tpu_custom_call" | custom-call | tf_op jit(solution)/shard_map/whole_step/pallas_call | solution.py:624
  37.7 1.4 %hand_on.1 = (f32[1,5]{1,0:T(1,128)}, f32[1,3,16,256]{3,2,1,0:T(8,128)}) custom-call(f32[1,5]{1,0:T(1,128)} %get-tuple-element.6.losses_ref, f32[1,3,16,256]{3,2,1,0:T(8,128)} %get-tuple-element.7.grads_ref), custom_call_target="tpu_custom_call" | custom-call | tf_op jit(solution)/shard_map/hand_on/pallas_call | solution.py:638

commit v3 on v2

--- a/solution.py
+++ b/solution.py
@@ -15,8 +15,7 @@
 CUBE = 0.044715
 
 ROWS = 8
-NZ = 8
-NY = 4
+DP = 32
 
 
 def dot(a, b):
@@ -108,24 +107,19 @@
     act1, sl1, act2, sl2, act3, sl3,
     a1, s1, a2, s2, a3, s3, a4, s4,
     stage0, land0, stage5, land5, stage4, land4,
-    parts, own, lrow, lz, ly,
+    parts, own, lrow, lall,
     wsem, ssem, rsem, gsend, grecv, lsend, lrecv,
 ):
     dp = lax.axis_index("dp")
     me = lax.axis_index("rows")
-    zi = lax.rem(dp, NZ)
-    yi = lax.div(dp, NZ)
     not_first = me > 0
     not_last = me < ROWS - 1
 
     def row_peer(k):
         return (dp, lax.rem(me + k, ROWS))
 
-    def z_peer(k):
-        return (yi * NZ + lax.rem(zi + k, NZ), me)
-
-    def y_peer(k):
-        return (lax.rem(yi + k, NY) * NZ + zi, me)
+    def dp_peer(k):
+        return (lax.rem(dp + k, DP), me)
 
     cw2 = [
         pltpu.make_async_copy(
@@ -140,11 +134,7 @@
         c.start()
 
     barrier = pltpu.get_barrier_semaphore()
-    peers = (
-        [row_peer(k) for k in range(1, ROWS)]
-        + [z_peer(k) for k in range(1, NZ)]
-        + [y_peer(k) for k in range(1, NY)]
-    )
+    peers = [row_peer(k) for k in range(1, ROWS)] + [dp_peer(k) for k in range(1, DP)]
     for peer in peers:
         pl.semaphore_signal(barrier, inc=1, device_id=peer, device_id_type=MESH)
 
@@ -233,11 +223,6 @@
     mine = stage0[...]
     patches(0, mine, ())
 
-    pl.semaphore_wait(barrier, len(peers))
-    c0 = beside(stage0, stage0, land0, 0)
-    for c in c0:
-        c.start()
-
     lane = iota((128, 128), 1)
     bias1 = vec[0:1, :]
     lin1 = vec[1:2, :]
@@ -256,15 +241,8 @@
         else:
             act_f, slope = gelu_both(pre[128:256])
             act = rounded(jnp.concatenate([gelu(pre[0:128]), act_f], axis=0))
-            if keep == "left":
-                act1[8, :, 0:128] = act[:, 128:256].astype(BF)
-                sl1[8, :, 0:128] = slope[:, 128:256]
-            elif keep == "right":
-                act1[8, :, 128:256] = act[:, 0:128].astype(BF)
-                sl1[8, :, 128:256] = slope[:, 0:128]
-            else:
-                act1[k] = act.astype(BF)
-                sl1[k] = slope
+            act1[keep] = act.astype(BF)
+            sl1[keep] = slope
         s = act[:, 0:128] + act[:, 128:256]
         v = rounded((s + pltpu.roll(s, 64, 1)) * 0.25)
         if ok is not None:
@@ -273,16 +251,24 @@
 
     def tap1(k, counted):
         act = act1[k].astype(F32)
+        slope = sl1[k]
+        if k == 8:
+            act = jnp.concatenate([act[:, 128:256], act1[9, :, 0:128].astype(F32)], axis=1)
+            slope = jnp.concatenate([slope[:, 128:256], sl1[9, :, 0:128]], axis=1)
         terms, grad = tap(act[0:128], act[128:256], lin1, sum_part)
         if counted:
             parts[0] += fold(terms)
-        slope = sl1[k]
         a1[k] = slope * grad
         s1[k] = slope * 0.25
 
     for k in range(1, 7):
-        segment1(0, k, 7 + k, "own", None)
-    for k in range(1, 7):
+        segment1(0, k, 7 + k, k, None)
+
+    pl.semaphore_wait(barrier, len(peers))
+    c0 = beside(stage0, stage0, land0, 0)
+    for c in c0:
+        c.start()
+    for k in range(1, 5):
         tap1(k, True)
 
     for c in cw2:
@@ -293,21 +279,22 @@
             w2t[ky, 0:64, kx * 128 : (kx + 1) * 128] = piece
             w2t[ky, 64:128, kx * 128 : (kx + 1) * 128] = piece
 
-    for c in c0:
-        c.wait()
-    upper = land0[0]
-    lower = land0[1]
-    patches(1, mine, ((upper, 15, 0, not_first), (lower, 0, 3, not_last)))
-    patches(2, upper, ((mine, 0, 3, None),))
-    patches(3, lower, ((mine, 15, 0, None),))
-    segment1(2, 7, 6, "left", not_first)
-    segment1(1, 0, 7, "own", None)
-    segment1(1, 7, 14, "own", None)
-    segment1(3, 0, 15, "right", not_last)
-
-    for k in range(1, 7):
-        segment1(2, k, k - 1, None, not_first)
-        segment1(3, k, 15 + k, None, not_last)
+    def edge1(side, slot):
+        pltpu.make_async_remote_copy(
+            src_ref=stage0, dst_ref=land0.at[side], send_sem=ssem.at[0, 0],
+            recv_sem=rsem.at[0, side], device_id=row_peer(1), device_id_type=MESH,
+        ).wait_recv()
+        ok = ((side == 0) & not_first) | ((side == 1) & not_last)
+        other = land0[side]
+        patches(slot, mine, ((other, 15 * (1 - side), 3 * side, ok),))
+        patches(slot + 1, other, ((mine, 15 * side, 3 * (1 - side), None),))
+        segment1(slot, 7 * side, 7 + 7 * side, 7 * side, None)
+        segment1(slot + 1, 7 * (1 - side), 6 + 9 * side, 8 + side, ok)
+        for k in range(1, 7):
+            segment1(slot + 1, k, k - 1 + 16 * side, None, ok)
+
+    near = 1 - lax.rem(me, 2)
+    edge1(near, 1)
 
     def put(ref, row, v, phases, c):
         n = phases * 16
@@ -332,23 +319,22 @@
     def segment2(m):
         pre = b2_ref[...]
         for ky in range(3):
-            rows = x2[2 * m + ky : 2 * m + ky + 2].reshape(512, 256)
+            rows = x2[pl.ds(2 * m + ky, 2)].reshape(512, 256)
             pre = pre + dot(rows, w2s[ky])
-        if 2 <= m < 8:
-            act, slope = both(pre, 128)
-            act2[m - 2] = act.astype(BF)
-            sl2[m - 2] = slope
-        else:
-            act = rounded(gelu(pre))
+        act, slope = both(pre, 128)
+        act2[m] = act.astype(BF)
+        sl2[m] = slope
         v = rounded(pool_cols(act[0:256] + act[256:512], 16) * 0.25)
-        if m < 3:
-            v = jnp.where(not_first, v, 0.0)
-        if m >= 7:
-            v = jnp.where(not_last, v, 0.0)
-        put(x3, m, v, 4, 128)
-
-    for m in range(10):
-        segment2(m)
+        ok = ((m >= 3) | not_first) & ((m < 7) | not_last)
+        put(x3, m, jnp.where(ok, v, 0.0), 4, 128)
+
+    for i in range(6):
+        segment2(4 * near + i)
+    edge1(1 - near, 3)
+    for i in range(4):
+        segment2(6 * (1 - near) + i)
+    for c in c0:
+        c.wait_send()
 
     cw3.wait()
 
@@ -415,8 +401,8 @@
         s3[2 * n : 2 * n + 2] = (slope * 0.25).reshape(2, 64, 256)
 
     def tap2(m, counted):
-        act = act2[m - 2].astype(F32).reshape(2, 2, 128, 128)
-        slope = sl2[m - 2]
+        act = act2[m].astype(F32).reshape(2, 2, 128, 128)
+        slope = sl2[m]
         terms, grad = tap(
             act[:, 0].reshape(256, 128), act[:, 1].reshape(256, 128), l2_ref[...], sum_full
         )
@@ -425,8 +411,8 @@
         a2[2 * m - 4 : 2 * m - 2] = (slope * (4.0 * grad)).reshape(2, 128, 128)
         s2[2 * m - 4 : 2 * m - 2] = (slope * 0.25).reshape(2, 128, 128)
 
-    tap1(0, True)
-    tap1(7, True)
+    for k in (5, 6, 0, 7):
+        tap1(k, True)
     tap1(8, False)
     tap3(1, True)
     tap3(2, True)
@@ -497,7 +483,7 @@
         put_back(g5, row + 2, gpre[row * 16 : (row + 1) * 16], 1, 512)
     fifth = jnp.sum(fold(terms), axis=0, keepdims=True)
     own[1] = gathered_loss(cl, lrow, ROWS) + jnp.where(rows_of == 4, fifth, 0.0)
-    cl = spread_loss(own.at[1], lz, zi, z_peer, NZ, 8)
+    cl = spread_loss(own.at[1], lall, dp, dp_peer, DP, 8)
 
     gin = jnp.zeros((48, 512), F32)
     for ky in range(3):
@@ -539,8 +525,6 @@
         for kx in range(3):
             n = (ky * 3 + kx) * 128
             gin = gin + dot_t(rows[:, kx * 256 : (kx + 1) * 256], w3s[n : n + 128, :])
-    own[2] = gathered_loss(cl, lz, NZ)
-    cl = spread_loss(own.at[2], ly, yi, y_peer, NY, 16)
 
     for j in range(12):
         wide = spread_cols(gin[(j // 2) * 64 : (j // 2 + 1) * 64], 4)
@@ -580,7 +564,7 @@
     out = dot(high, back) + dot(low, back)
     grad_ref[0] = out[0:48].reshape(3, 16, 256)
 
-    total = gathered_loss(cl, ly, NY)
+    total = gathered_loss(cl, lall, DP)
     sums = jnp.sum(total, axis=1, keepdims=True)
     lanes = iota((8, 128), 1)
     counts = [32.0 * (128 >> s) * (256 >> s) for s in range(5)]
@@ -606,20 +590,19 @@
     scratch = [
         v((3, 256, 128), BF), v((3, 128, 384), BF), v((1152, 256), BF), v((2304, 512), BF),
         v((4608, 512), BF), v((16, 512), F32), v((9, 256, 256), BF), v((8, 256), F32),
-        v((4, 256, 256), BF),
+        v((5, 256, 256), BF),
         v((22, 256, 256), BF), v((10, 128, 384), BF), v((4, 64, 768), BF), v((10, 32, 1536), BF),
         v((12, 128, 384), BF), v((8, 64, 768), BF), v((6, 32, 1536), BF), v((12, 16, 1536), BF),
         v((9, 128, 256), BF),
-        v((9, 256, 256), BF), v((9, 128, 256), F32), v((6, 512, 128), BF),
-        v((6, 256, 128), F32), v((4, 256, 256), BF), v((4, 128, 256), F32),
+        v((10, 256, 256), BF), v((10, 128, 256), F32), v((10, 512, 128), BF),
+        v((10, 256, 128), F32), v((4, 256, 256), BF), v((4, 128, 256), F32),
         v((9, 128, 256), F32), v((9, 128, 256), F32), v((12, 128, 128), F32),
         v((12, 128, 128), F32), v((8, 64, 256), F32), v((8, 64, 256), F32),
         v((2, 32, 512), F32), v((2, 32, 512), F32),
         v((96, 256), BF), v((2, 96, 256), BF), v((32, 512), BF), v((8, 32, 512), BF),
         v((4, 32, 512), BF), v((2, 4, 32, 512), BF),
-        v((5, 8, 128), F32), v((3, 8, 128), F32), v((8, 8, 128), F32), v((8, 8, 128), F32),
-        v((4, 8, 128), F32),
-        dma((6,)), dma((2, 2)), dma((2, 2)), dma((7,)), dma((7,)), dma((24,)), dma((24,)),
+        v((5, 8, 128), F32), v((2, 8, 128), F32), v((8, 8, 128), F32), v((32, 8, 128), F32),
+        dma((6,)), dma((2, 2)), dma((2, 2)), dma((7,)), dma((7,)), dma((40,)), dma((40,)),
     ]
     losses, grads = pl.pallas_call(
         body,

time: 39.3 us -> 40.6 us (1.033)
  Pallas kernels: 38.5 us -> 39.7 us
    pallas_call x1, Pallas kernels: 37 us -> 38.3 us  [on_device(): pl.pallas_call(body, out_shape=(jax.ShapeDtypeStruct((1, 5), F32), jax.Sh...]
where the time goes in v3:
time: 40.6 us; the launch traced here: 40.4 us
  Pallas kernels  39.7 us (98%)
  between operations  0.65 us (2%)
    pallas_call x1, Pallas kernels, on_device(): pl.pallas_call(body, out_shape=(jax.ShapeDtypeStruct((1, 5), F32), jax.Sh...  38.3 us
    pallas_call x1, Pallas kernels, on_device(): pl.pallas_call(hand_on, out_shape=(jax.ShapeDtypeStruct((1, 5), F32), jax...  1.43 us

profile of v3, /device:TPU:1, one launch (start us, length us, event | category | flops | bytes accessed | tf_op | source)
XLA Modules:
  0.0 40.4 jit_solution(15098191626264476922)
XLA Ops:
  0.6 38.3 %whole_step.1 = (f32[1,5]{1,0:T(1,128)}, f32[1,3,16,256]{3,2,1,0:T(8,128)}) custom-call(bf16[1,3,16,256]{3,2,1,0:T(8,128)(2,1)} %real_ref.1, bf16[1,3,16,256]{3,2,1,0:T(8,128)(2,1)} %fake_ref.1, bf16[3,3,3,64]{3,2,1,0:T(4,128)(2,1)} %w1_ref.1, bf16[576,128]{1,0:T(8,128)(2,1)} %bitcast.18, bf16[1152,256]{1,0:T(8,128)(2,1)} %bitcast.17, ...), custom_call_target="tpu_custom_call" | custom-call | tf_op jit(solution)/shard_map/whole_step/pallas_call | solution.py:607
  39.0 1.4 %hand_on.1 = (f32[1,5]{1,0:T(1,128)}, f32[1,3,16,256]{3,2,1,0:T(8,128)}) custom-call(f32[1,5]{1,0:T(1,128)} %get-tuple-element.6.losses_ref, f32[1,3,16,256]{3,2,1,0:T(8,128)} %get-tuple-element.7.grads_ref), custom_call_target="tpu_custom_call" | custom-call | tf_op jit(solution)/shard_map/hand_on/pallas_call | solution.py:621

commit v4 on v2

--- a/solution.py
+++ b/solution.py
@@ -104,7 +104,7 @@
     b1_ref, b2_ref, b3_ref, b4_ref, b5_ref, l1_ref, l2_ref, l3_ref, l4_ref, l5_ref,
     loss_ref, grad_ref,
     w2s, w2t, w3s, w4s, w5s, wsm, wb, vec, tt,
-    x2, x3, x4, x5, g2, g3, g4, g5, gp1,
+    x2, x3, x4, x5, g2, g3, g4, g5, back,
     act1, sl1, act2, sl2, act3, sl3,
     a1, s1, a2, s2, a3, s3, a4, s4,
     stage0, land0, stage5, land5, stage4, land4,
@@ -129,13 +129,16 @@
 
     cw2 = [
         pltpu.make_async_copy(
-            w2_hbm.at[pl.ds(ky * 192, 192)], w2s.at[ky, pl.ds(0, 192)], wsem.at[ky]
+            w2_hbm.at[pl.ds(ky * 192, 192)],
+            w2s.at[ky + half, pl.ds(0, 192), pl.ds(half * 128, 128)],
+            wsem.at[2 * ky + half],
         )
         for ky in range(3)
+        for half in range(2)
     ]
-    cw3 = pltpu.make_async_copy(w3_hbm, w3s, wsem.at[3])
-    cw4 = pltpu.make_async_copy(w4_hbm, w4s, wsem.at[4])
-    cw5 = pltpu.make_async_copy(w5_hbm, w5s, wsem.at[5])
+    cw3 = pltpu.make_async_copy(w3_hbm, w3s, wsem.at[6])
+    cw4 = pltpu.make_async_copy(w4_hbm, w4s, wsem.at[7])
+    cw5 = pltpu.make_async_copy(w5_hbm, w5s, wsem.at[8])
     for c in cw2 + [cw3, cw4, cw5]:
         c.start()
 
@@ -191,22 +194,29 @@
     for row, ref in ((0, b1_ref), (1, l1_ref)):
         for q in range(4):
             vec[row : row + 1, q * 64 : (q + 1) * 64] = ref[...]
+    for row, ref in ((2, b2_ref), (3, l2_ref)):
+        for q in range(2):
+            vec[row : row + 1, q * 128 : (q + 1) * 128] = ref[...]
     ones_part = onehot(iota((256, 256), 0) >> 6 == iota((256, 256), 1) >> 6)
-    ones_full = jnp.full((128, 128), 1.0, BF)
+    ones_rows = onehot(iota((256, 256), 0) >> 7 == iota((256, 256), 1) >> 7)
 
     def sum_part(x):
         return dot(x.astype(BF), ones_part)
 
-    def sum_full(x):
-        return dot(x.astype(BF), ones_full)
+    def sum_rows(x):
+        return dot(x.astype(BF), ones_rows)
 
     parts[...] = jnp.zeros_like(parts)
-    w2s[:, 192:256, :] = jnp.zeros((3, 64, 128), BF)
+    w2s[:, 192:256, :] = jnp.zeros((4, 64, 256), BF)
+    w2s[0, 0:192, 128:256] = jnp.zeros((192, 128), BF)
+    w2s[3, 0:192, 0:128] = jnp.zeros((192, 128), BF)
 
     pos = iota((128, 256), 0)
     col = iota((128, 256), 1)
     base = 16 * (pos & 15) + 2 * (pos >> 4)
     take = onehot(col == base)
+    for d in range(4):
+        back[d * 128 : (d + 1) * 128, :] = onehot(col == base + d - 1)
 
     def patches(slot, images, sources):
         for i in range(2):
@@ -287,12 +297,43 @@
 
     for c in cw2:
         c.wait()
-    for ky in range(3):
+    for at, ky in ((0, 0), (64, 2), (128, 1), (192, 1)):
         for kx in range(3):
-            piece = w2s[ky, kx * 64 : (kx + 1) * 64, :]
-            w2t[ky, 0:64, kx * 128 : (kx + 1) * 128] = piece
-            w2t[ky, 64:128, kx * 128 : (kx + 1) * 128] = piece
-
+            piece = w2s[ky, kx * 64 : (kx + 1) * 64, 0:128]
+            w2t[at : at + 64, kx * 128 : (kx + 1) * 128] = piece
+
+    def put(ref, row, v, phases, c):
+        n = phases * 16
+        for i in range(2):
+            w = v[i * n : (i + 1) * n]
+            left, right = shifted(w, phases)
+            ref[row, i * n : (i + 1) * n, 0:c] = left.astype(BF)
+            ref[row, i * n : (i + 1) * n, c : 2 * c] = w.astype(BF)
+            ref[row, i * n : (i + 1) * n, 2 * c : 3 * c] = right.astype(BF)
+
+    bias2 = vec[2:3, :]
+    lin2 = vec[3:4, :]
+
+    def segment2(m):
+        pre = bias2
+        for d in range(4):
+            pre = pre + dot(x2[2 * m + d], w2s[d])
+        if 2 <= m < 8:
+            act_f, slope = gelu_both(pre[128:256])
+            act = rounded(jnp.concatenate([gelu(pre[0:128]), act_f], axis=0))
+            act2[m - 2] = act.astype(BF)
+            sl2[m - 2] = slope
+        else:
+            act = rounded(gelu(pre))
+        v = rounded(pool_cols(act[:, 0:128] + act[:, 128:256], 16) * 0.25)
+        if m < 3:
+            v = jnp.where(not_first, v, 0.0)
+        if m >= 7:
+            v = jnp.where(not_last, v, 0.0)
+        put(x3, m, v, 4, 128)
+
+    segment2(4)
+    segment2(5)
     for c in c0:
         c.wait()
     upper = land0[0]
@@ -309,14 +350,8 @@
         segment1(2, k, k - 1, None, not_first)
         segment1(3, k, 15 + k, None, not_last)
 
-    def put(ref, row, v, phases, c):
-        n = phases * 16
-        for i in range(2):
-            w = v[i * n : (i + 1) * n]
-            left, right = shifted(w, phases)
-            ref[row, i * n : (i + 1) * n, 0:c] = left.astype(BF)
-            ref[row, i * n : (i + 1) * n, c : 2 * c] = w.astype(BF)
-            ref[row, i * n : (i + 1) * n, 2 * c : 3 * c] = right.astype(BF)
+    for m in (0, 1, 2, 3, 6, 7, 8, 9):
+        segment2(m)
 
     def both(pre, n):
         parts_of = []
@@ -329,34 +364,11 @@
             slopes.append(slope)
         return rounded(jnp.concatenate(parts_of, axis=0)), jnp.concatenate(slopes, axis=0)
 
-    def segment2(m):
-        pre = b2_ref[...]
-        for ky in range(3):
-            rows = x2[2 * m + ky : 2 * m + ky + 2].reshape(512, 256)
-            pre = pre + dot(rows, w2s[ky])
-        if 2 <= m < 8:
-            act, slope = both(pre, 128)
-            act2[m - 2] = act.astype(BF)
-            sl2[m - 2] = slope
-        else:
-            act = rounded(gelu(pre))
-        v = rounded(pool_cols(act[0:256] + act[256:512], 16) * 0.25)
-        if m < 3:
-            v = jnp.where(not_first, v, 0.0)
-        if m >= 7:
-            v = jnp.where(not_last, v, 0.0)
-        put(x3, m, v, 4, 128)
-
-    for m in range(10):
-        segment2(m)
-
     cw3.wait()
 
     def segment3(n):
-        pre = b3_ref[...]
-        for ky in range(3):
-            rows = x3[2 * n + ky : 2 * n + ky + 2].reshape(256, 384)
-            pre = pre + dot(rows, w3s[ky * 384 : (ky + 1) * 384, :])
+        rows = [x3[2 * n + ky : 2 * n + ky + 2].reshape(256, 384) for ky in range(3)]
+        pre = dot(jnp.concatenate(rows, axis=1), w3s[...]) + b3_ref[...]
         act, slope = both(pre, 64)
         act3[n] = act.astype(BF)
         sl3[n] = slope
@@ -415,15 +427,13 @@
         s3[2 * n : 2 * n + 2] = (slope * 0.25).reshape(2, 64, 256)
 
     def tap2(m, counted):
-        act = act2[m - 2].astype(F32).reshape(2, 2, 128, 128)
+        act = act2[m - 2].astype(F32)
         slope = sl2[m - 2]
-        terms, grad = tap(
-            act[:, 0].reshape(256, 128), act[:, 1].reshape(256, 128), l2_ref[...], sum_full
-        )
+        terms, grad = tap(act[0:128], act[128:256], lin2, sum_rows)
         if counted:
             parts[1] += fold(terms)
-        a2[2 * m - 4 : 2 * m - 2] = (slope * (4.0 * grad)).reshape(2, 128, 128)
-        s2[2 * m - 4 : 2 * m - 2] = (slope * 0.25).reshape(2, 128, 128)
+        a2[m - 2] = slope * (4.0 * grad)
+        s2[m - 2] = slope * 0.25
 
     tap1(0, True)
     tap1(7, True)
@@ -544,40 +554,40 @@
 
     for j in range(12):
         wide = spread_cols(gin[(j // 2) * 64 : (j // 2 + 1) * 64], 4)
-        v = a2[j] + s2[j] * wide
+        at = (j % 2) * 128
+        v = a2[j // 2, :, at : at + 128] + s2[j // 2, :, at : at + 128] * wide
         if j < 2:
             v = jnp.where(not_first, v, 0.0)
         if j >= 10:
             v = jnp.where(not_last, v, 0.0)
         put_back(g2, j, rounded(v), 8, 128)
 
-    for n in range(4):
-        g = 0.0
-        for ky in range(3):
-            rows = g2[2 * n + 3 - ky : 2 * n + 5 - ky].reshape(256, 384)
-            g = g + dot_t(rows, w2t[ky])
-        for j in range(2):
-            k = 2 * n + j
-            one = g[j * 128 : (j + 1) * 128]
-            wide = jnp.concatenate([one, one], axis=1)
-            gp1[k] = (a1[k] + s1[k] * wide).astype(BF)
-    g = 0.0
-    for ky in range(3):
-        rows = jnp.concatenate([g2[2 - ky], g2[11 - ky]], axis=0)
-        g = g + dot_t(rows, w2t[ky])
-    above = jnp.where(not_first, a1[8, :, 0:128] + s1[8, :, 0:128] * g[0:128], 0.0)
-    below = jnp.where(not_last, a1[8, :, 128:256] + s1[8, :, 128:256] * g[128:256], 0.0)
-    gp1[8] = jnp.concatenate([above, below], axis=1).astype(BF)
-
-    g = jnp.zeros((128, 256), F32)
+    products = []
+    for n in range(6):
+        two = dot_t(g2[2 * n : 2 * n + 2].reshape(256, 384), w2t[...])
+        products += [two[0:128], two[128:256]]
+
+    def gin2(z):
+        u = jnp.where(lane < 64, products[z + 2][:, 0:128], products[z][:, 0:128])
+        return u + pltpu.roll(u, 64, 1) + products[z + 1][:, 128:256]
+
+    across = jnp.zeros((256, 128), F32)
     for k in range(9):
-        g = g + dot_t(gp1[k], wb[k])
-    across = jnp.transpose(g)
+        if k < 8:
+            g = gin2(k + 1)
+            wide = jnp.concatenate([g, g], axis=1)
+            v = a1[k] + s1[k] * wide
+        else:
+            above = a1[8, :, 0:128] + s1[8, :, 0:128] * gin2(0)
+            below = a1[8, :, 128:256] + s1[8, :, 128:256] * gin2(9)
+            v = jnp.concatenate(
+                [jnp.where(not_first, above, 0.0), jnp.where(not_last, below, 0.0)], axis=1
+            )
+        across = across + dot_t(wb[k], v.astype(BF))
     lined = jnp.concatenate([across[d * 64 : (d + 1) * 64] for d in range(4)], axis=1)
-    back = jnp.concatenate([onehot(col == base + d - 1) for d in range(4)], axis=0)
     high = lined.astype(BF)
     low = (lined - high.astype(F32)).astype(BF)
-    out = dot(high, back) + dot(low, back)
+    out = dot(high, back[...]) + dot(low, back[...])
     grad_ref[0] = out[0:48].reshape(3, 16, 256)
 
     total = gathered_loss(cl, ly, NY)
@@ -604,22 +614,22 @@
     v = pltpu.VMEM
     dma = pltpu.SemaphoreType.DMA
     scratch = [
-        v((3, 256, 128), BF), v((3, 128, 384), BF), v((1152, 256), BF), v((2304, 512), BF),
+        v((4, 256, 256), BF), v((256, 384), BF), v((1152, 256), BF), v((2304, 512), BF),
         v((4608, 512), BF), v((16, 512), F32), v((9, 256, 256), BF), v((8, 256), F32),
         v((4, 256, 256), BF),
         v((22, 256, 256), BF), v((10, 128, 384), BF), v((4, 64, 768), BF), v((10, 32, 1536), BF),
         v((12, 128, 384), BF), v((8, 64, 768), BF), v((6, 32, 1536), BF), v((12, 16, 1536), BF),
-        v((9, 128, 256), BF),
-        v((9, 256, 256), BF), v((9, 128, 256), F32), v((6, 512, 128), BF),
-        v((6, 256, 128), F32), v((4, 256, 256), BF), v((4, 128, 256), F32),
-        v((9, 128, 256), F32), v((9, 128, 256), F32), v((12, 128, 128), F32),
-        v((12, 128, 128), F32), v((8, 64, 256), F32), v((8, 64, 256), F32),
+        v((512, 256), BF),
+        v((9, 256, 256), BF), v((9, 128, 256), F32), v((6, 256, 256), BF),
+        v((6, 128, 256), F32), v((4, 256, 256), BF), v((4, 128, 256), F32),
+        v((9, 128, 256), F32), v((9, 128, 256), F32), v((6, 128, 256), F32),
+        v((6, 128, 256), F32), v((8, 64, 256), F32), v((8, 64, 256), F32),
         v((2, 32, 512), F32), v((2, 32, 512), F32),
         v((96, 256), BF), v((2, 96, 256), BF), v((32, 512), BF), v((8, 32, 512), BF),
         v((4, 32, 512), BF), v((2, 4, 32, 512), BF),
         v((5, 8, 128), F32), v((3, 8, 128), F32), v((8, 8, 128), F32), v((8, 8, 128), F32),
         v((4, 8, 128), F32),
-        dma((6,)), dma((2, 2)), dma((2, 2)), dma((7,)), dma((7,)), dma((24,)), dma((24,)),
+        dma((9,)), dma((2, 2)), dma((2, 2)), dma((7,)), dma((7,)), dma((24,)), dma((24,)),
     ]
     losses, grads = pl.pallas_call(
         body,

time: 39.3 us -> 39.1 us (level)
  no operation moved by 1% of the time
where the time goes in v4:
time: 39.1 us; the launch traced here: 38.9 us
  Pallas kernels  38.3 us (98%)
  between operations  0.65 us (2%)
    pallas_call x1, Pallas kernels, on_device(): pl.pallas_call(body, out_shape=(jax.ShapeDtypeStruct((1, 5), F32), jax.Sh...  36.9 us
    pallas_call x1, Pallas kernels, on_device(): pl.pallas_call(hand_on, out_shape=(jax.ShapeDtypeStruct((1, 5), F32), jax...  1.43 us

profile of v4, /device:TPU:1, one launch (start us, length us, event | category | flops | bytes accessed | tf_op | source)
XLA Modules:
  0.0 38.9 jit_solution(18292759863925970996)
XLA Ops:
  0.6 36.9 %whole_step.1 = (f32[1,5]{1,0:T(1,128)}, f32[1,3,16,256]{3,2,1,0:T(8,128)}) custom-call(bf16[1,3,16,256]{3,2,1,0:T(8,128)(2,1)} %real_ref.1, bf16[1,3,16,256]{3,2,1,0:T(8,128)(2,1)} %fake_ref.1, bf16[3,3,3,64]{3,2,1,0:T(4,128)(2,1)} %w1_ref.1, bf16[576,128]{1,0:T(8,128)(2,1)} %bitcast.18, bf16[1152,256]{1,0:T(8,128)(2,1)} %bitcast.17, ...), custom_call_target="tpu_custom_call" | custom-call | tf_op jit(solution)/shard_map/whole_step/pallas_call | solution.py:634
  37.5 1.4 %hand_on.1 = (f32[1,5]{1,0:T(1,128)}, f32[1,3,16,256]{3,2,1,0:T(8,128)}) custom-call(f32[1,5]{1,0:T(1,128)} %get-tuple-element.6.losses_ref, f32[1,3,16,256]{3,2,1,0:T(8,128)} %get-tuple-element.7.grads_ref), custom_call_target="tpu_custom_call" | custom-call | tf_op jit(solution)/shard_map/hand_on/pallas_call | solution.py:648

commit v5 on v4

--- a/solution.py
+++ b/solution.py
@@ -39,17 +39,17 @@
     return x.astype(BF).astype(F32)
 
 
-def gelu(x):
-    t = jnp.tanh(x * (ROOT + (ROOT * CUBE) * (x * x)))
-    return x * (0.5 + 0.5 * t)
-
-
-def gelu_both(x):
-    x2 = x * x
-    t = jnp.tanh(x * (ROOT + (ROOT * CUBE) * x2))
-    h = 0.5 + 0.5 * t
-    slope = h + (0.5 * x) * (1.0 - t * t) * (ROOT + (3.0 * ROOT * CUBE) * x2)
-    return x * h, slope
+def gelu(h):
+    t = jnp.tanh(h * (2.0 * ROOT + (8.0 * ROOT * CUBE) * (h * h)))
+    return h + h * t
+
+
+def gelu_both(h):
+    h2 = h * h
+    t = jnp.tanh(h * (2.0 * ROOT + (8.0 * ROOT * CUBE) * h2))
+    ht = h * t
+    slope = (0.5 + 0.5 * t) + (h - ht * t) * (ROOT + (12.0 * ROOT * CUBE) * h2)
+    return h + ht, slope
 
 
 def tap(r, f, lin, total):
@@ -100,16 +100,18 @@
 
 
 def body(
-    real_ref, fake_ref, w1_ref, w2_hbm, w3_hbm, w4_hbm, w5_hbm,
+    real_hbm, fake_hbm, w1_hbm, w2_hbm, w3_hbm, w4_hbm, w5_hbm,
+    b1_hbm, b2_hbm, b3_hbm, b4_hbm, b5_hbm, l1_hbm, l2_hbm, l3_hbm, l4_hbm, l5_hbm,
+    loss_ref, grad_ref,
+    real_ref, fake_ref, w1_ref,
     b1_ref, b2_ref, b3_ref, b4_ref, b5_ref, l1_ref, l2_ref, l3_ref, l4_ref, l5_ref,
-    loss_ref, grad_ref,
     w2s, w2t, w3s, w4s, w5s, wsm, wb, vec, tt,
     x2, x3, x4, x5, g2, g3, g4, g5, back,
     act1, sl1, act2, sl2, act3, sl3,
     a1, s1, a2, s2, a3, s3, a4, s4,
     stage0, land0, stage5, land5, stage4, land4,
     parts, own, lrow, lz, ly,
-    wsem, ssem, rsem, gsend, grecv, lsend, lrecv,
+    isem, wsem, ssem, rsem, gsend, grecv, lsend, lrecv,
 ):
     dp = lax.axis_index("dp")
     me = lax.axis_index("rows")
@@ -126,6 +128,26 @@
 
     def y_peer(k):
         return (lax.rem(yi + k, NY) * NZ + zi, me)
+
+    barrier = pltpu.get_barrier_semaphore()
+    peers = (
+        [row_peer(k) for k in range(1, ROWS)]
+        + [z_peer(k) for k in range(1, NZ)]
+        + [y_peer(k) for k in range(1, NY)]
+    )
+    for peer in peers:
+        pl.semaphore_signal(barrier, inc=1, device_id=peer, device_id_type=MESH)
+
+    small_inputs = (
+        (real_hbm, real_ref), (fake_hbm, fake_ref), (w1_hbm, w1_ref),
+        (b1_hbm, b1_ref), (b2_hbm, b2_ref), (b3_hbm, b3_ref), (b4_hbm, b4_ref), (b5_hbm, b5_ref),
+        (l1_hbm, l1_ref), (l2_hbm, l2_ref), (l3_hbm, l3_ref), (l4_hbm, l4_ref), (l5_hbm, l5_ref),
+    )
+    ci = [
+        pltpu.make_async_copy(src, dst, isem.at[n]) for n, (src, dst) in enumerate(small_inputs)
+    ]
+    for c in ci:
+        c.start()
 
     cw2 = [
         pltpu.make_async_copy(
@@ -142,14 +164,6 @@
     for c in cw2 + [cw3, cw4, cw5]:
         c.start()
 
-    barrier = pltpu.get_barrier_semaphore()
-    peers = (
-        [row_peer(k) for k in range(1, ROWS)]
-        + [z_peer(k) for k in range(1, NZ)]
-        + [y_peer(k) for k in range(1, NY)]
-    )
-    for peer in peers:
-        pl.semaphore_signal(barrier, inc=1, device_id=peer, device_id_type=MESH)
 
     def beside(first, second, land, n):
         up = pltpu.make_async_remote_copy(
@@ -162,13 +176,15 @@
         )
         return up, down
 
+    for c in ci:
+        c.wait()
     stage0[0:48] = real_ref[0].reshape(48, 256)
     stage0[48:96] = fake_ref[0].reshape(48, 256)
 
     wsm[...] = jnp.zeros_like(wsm)
     for ky in range(3):
         for kx in range(3):
-            piece = w1_ref[ky, kx].astype(F32)
+            piece = w1_ref[ky, kx].astype(F32) * 0.5
             for p in range(2):
                 lane = (kx + p) * 128 + p * 64
                 wsm[ky * 3 : ky * 3 + 3, lane : lane + 64] = piece
@@ -191,12 +207,12 @@
                     :, d * 128 : (d + 1) * 128
                 ]
 
-    for row, ref in ((0, b1_ref), (1, l1_ref)):
+    for row, ref, scale in ((0, b1_ref, 0.5), (1, l1_ref, 1.0)):
         for q in range(4):
-            vec[row : row + 1, q * 64 : (q + 1) * 64] = ref[...]
-    for row, ref in ((2, b2_ref), (3, l2_ref)):
+            vec[row : row + 1, q * 64 : (q + 1) * 64] = ref[...] * scale
+    for row, ref, scale in ((2, b2_ref, 0.5), (3, l2_ref, 1.0)):
         for q in range(2):
-            vec[row : row + 1, q * 128 : (q + 1) * 128] = ref[...]
+            vec[row : row + 1, q * 128 : (q + 1) * 128] = ref[...] * scale
     ones_part = onehot(iota((256, 256), 0) >> 6 == iota((256, 256), 1) >> 6)
     ones_rows = onehot(iota((256, 256), 0) >> 7 == iota((256, 256), 1) >> 7)
 
@@ -276,7 +292,7 @@
                 act1[k] = act.astype(BF)
                 sl1[k] = slope
         s = act[:, 0:128] + act[:, 128:256]
-        v = rounded((s + pltpu.roll(s, 64, 1)) * 0.25)
+        v = rounded((s + pltpu.roll(s, 64, 1)) * 0.125)
         if ok is not None:
             v = jnp.where(ok, v, 0.0)
         put2(p, v)
@@ -325,7 +341,7 @@
             sl2[m - 2] = slope
         else:
             act = rounded(gelu(pre))
-        v = rounded(pool_cols(act[:, 0:128] + act[:, 128:256], 16) * 0.25)
+        v = rounded(pool_cols(act[:, 0:128] + act[:, 128:256], 16) * 0.125)
         if m < 3:
             v = jnp.where(not_first, v, 0.0)
         if m >= 7:
@@ -368,11 +384,11 @@
 
     def segment3(n):
         rows = [x3[2 * n + ky : 2 * n + ky + 2].reshape(256, 384) for ky in range(3)]
-        pre = dot(jnp.concatenate(rows, axis=1), w3s[...]) + b3_ref[...]
+        pre = dot(jnp.concatenate(rows, axis=1), w3s[...]) + b3_ref[...] * 0.5
         act, slope = both(pre, 64)
         act3[n] = act.astype(BF)
         sl3[n] = slope
-        v = rounded(pool_cols(act[0:128] + act[128:256], 8) * 0.25)
+        v = rounded(pool_cols(act[0:128] + act[128:256], 8) * 0.125)
         if n < 1:
             v = jnp.where(not_first, v, 0.0)
         if n >= 3:
@@ -383,12 +399,12 @@
         segment3(n)
 
     cw4.wait()
-    pre = b4_ref[...]
+    pre = b4_ref[...] * 0.5
     for ky in range(3):
         rows = x4[ky : ky + 2].reshape(128, 768)
         pre = pre + dot(rows, w4s[ky * 768 : (ky + 1) * 768, :])
     act, slope = both(pre, 32)
-    stage5[...] = (pool_cols(act[0:64] + act[64:128], 4) * 0.25).astype(BF)
+    stage5[...] = (pool_cols(act[0:64] + act[64:128], 4) * 0.125).astype(BF)
     c5 = [
         pltpu.make_async_remote_copy(
             src_ref=stage5, dst_ref=land5.at[me], send_sem=gsend.at[k - 1],
@@ -486,7 +502,7 @@
         c.wait()
     for row in range(ROWS):
         put(x5, row + 1, land5[row].astype(F32), 1, 512)
-    pre = b5_ref[...]
+    pre = b5_ref[...] * 0.5
     for ky in range(3):
         rows = x5[ky : ky + 8].reshape(256, 1536)
         pre = pre + dot(rows, w5s[ky * 1536 : (ky + 1) * 1536, :])
@@ -584,6 +600,7 @@
                 [jnp.where(not_first, above, 0.0), jnp.where(not_last, below, 0.0)], axis=1
             )
         across = across + dot_t(wb[k], v.astype(BF))
+    across = across * 2.0
     lined = jnp.concatenate([across[d * 64 : (d + 1) * 64] for d in range(4)], axis=1)
     high = lined.astype(BF)
     low = (lined - high.astype(F32)).astype(BF)
@@ -613,7 +630,7 @@
     anywhere = pl.BlockSpec(memory_space=pl.ANY)
     v = pltpu.VMEM
     dma = pltpu.SemaphoreType.DMA
-    scratch = [
+    scratch = [v(a.shape, a.dtype) for a in (real, fake, w1, *vectors)] + [
         v((4, 256, 256), BF), v((256, 384), BF), v((1152, 256), BF), v((2304, 512), BF),
         v((4608, 512), BF), v((16, 512), F32), v((9, 256, 256), BF), v((8, 256), F32),
         v((4, 256, 256), BF),
@@ -629,15 +646,12 @@
         v((4, 32, 512), BF), v((2, 4, 32, 512), BF),
         v((5, 8, 128), F32), v((3, 8, 128), F32), v((8, 8, 128), F32), v((8, 8, 128), F32),
         v((4, 8, 128), F32),
-        dma((9,)), dma((2, 2)), dma((2, 2)), dma((7,)), dma((7,)), dma((24,)), dma((24,)),
+        dma((13,)), dma((9,)), dma((2, 2)), dma((2, 2)), dma((7,)), dma((7,)), dma((24,)), dma((24,)),
     ]
     losses, grads = pl.pallas_call(
         body,
-        out_shape=(
-            jax.ShapeDtypeStruct((1, 5), F32),
-            jax.ShapeDtypeStruct((1, 3, 16, 256), F32),
-        ),
-        in_specs=[vmem] * 3 + [anywhere] * 4 + [vmem] * 10,
+        out_shape=(v((1, 5), F32), v((1, 3, 16, 256), F32)),
+        in_specs=[anywhere] * 17,
         out_specs=(vmem, vmem),
         scratch_shapes=scratch,
         compiler_params=pltpu.CompilerParams(
@@ -654,7 +668,10 @@
         in_specs=[vmem] * 2,
         out_specs=(vmem, vmem),
         name="hand_on",
-    )(losses, grads)
+    )(
+        pltpu.with_memory_space_constraint(losses, pltpu.VMEM),
+        pltpu.with_memory_space_constraint(grads, pltpu.VMEM),
+    )
     return (losses.reshape(5), grads)
 
 

time: 39.1 us -> 36.7 us (0.939)
  Pallas kernels: 38.3 us -> 36 us
    pallas_call x1, Pallas kernels: 36.9 us -> 35.3 us  [on_device(): pl.pallas_call(body, out_shape=(v((1, 5), F32), v((1, 3, 16, 256), F32)),...]
    pallas_call x1, Pallas kernels: 1.43 us -> 0.63 us  [on_device(): pl.pallas_call(hand_on, out_shape=(jax.ShapeDtypeStruct((1, 5), F32), jax...]
where the time goes in v5:
time: 36.7 us; the launch traced here: 36.6 us
  Pallas kernels  36 us (98%)
  between operations  0.65 us (2%)
    pallas_call x1, Pallas kernels, on_device(): pl.pallas_call(body, out_shape=(v((1, 5), F32), v((1, 3, 16, 256), F32)),...  35.3 us

profile of v5, /device:TPU:1, one launch (start us, length us, event | category | flops | bytes accessed | tf_op | source)
XLA Modules:
  0.0 36.6 jit_solution(2564555488980204214)
XLA Ops:
  0.6 35.3 %whole_step.1 = (f32[1,5]{1,0:T(1,128)S(1)}, f32[1,3,16,256]{3,2,1,0:T(8,128)S(1)}) custom-call(bf16[1,3,16,256]{3,2,1,0:T(8,128)(2,1)} %real_hbm.1, bf16[1,3,16,256]{3,2,1,0:T(8,128)(2,1)} %fake_hbm.1, bf16[3,3,3,64]{3,2,1,0:T(4,128)(2,1)} %w1_hbm.1, bf16[576,128]{1,0:T(8,128)(2,1)} %bitcast.18, bf16[1152,256]{1,0:T(8,128)(2,1)} %bitcast.17, ...), custom_call_target="tpu_custom_call" | custom-call | tf_op jit(solution)/shard_map/whole_step/pallas_call | solution.py:651
  36.0 0.6 %hand_on.1 = (f32[1,5]{1,0:T(1,128)}, f32[1,3,16,256]{3,2,1,0:T(8,128)}) custom-call(f32[1,5]{1,0:T(1,128)S(1)} %get-tuple-element.6.losses_ref, f32[1,3,16,256]{3,2,1,0:T(8,128)S(1)} %get-tuple-element.7.grads_ref), custom_call_target="tpu_custom_call" | custom-call | tf_op jit(solution)/shard_map/hand_on/pallas_call | solution.py:662

commit v6 on v5

--- a/solution.py
+++ b/solution.py
@@ -50,6 +50,12 @@
     ht = h * t
     slope = (0.5 + 0.5 * t) + (h - ht * t) * (ROOT + (12.0 * ROOT * CUBE) * h2)
     return h + ht, slope
+
+
+def slope_of(h):
+    h2 = h * h
+    t = jnp.tanh(h * (2.0 * ROOT + (8.0 * ROOT * CUBE) * h2))
+    return (0.5 + 0.5 * t) + (h - h * t * t) * (ROOT + (12.0 * ROOT * CUBE) * h2)
 
 
 def tap(r, f, lin, total):
@@ -277,11 +283,9 @@
 
     def segment1(slot, k, p, keep, ok):
         pre = dot(tt[slot], wb[k]) + bias1
-        if keep is None:
-            act = rounded(gelu(pre))
-        else:
-            act_f, slope = gelu_both(pre[128:256])
-            act = rounded(jnp.concatenate([gelu(pre[0:128]), act_f], axis=0))
+        act = rounded(gelu(pre))
+        if keep is not None:
+            slope = pre[128:256]
             if keep == "left":
                 act1[8, :, 0:128] = act[:, 128:256].astype(BF)
                 sl1[8, :, 0:128] = slope[:, 128:256]
@@ -302,7 +306,7 @@
         terms, grad = tap(act[0:128], act[128:256], lin1, sum_part)
         if counted:
             parts[0] += fold(terms)
-        slope = sl1[k]
+        slope = slope_of(sl1[k])
         a1[k] = slope * grad
         s1[k] = slope * 0.25
 
@@ -334,13 +338,10 @@
         pre = bias2
         for d in range(4):
             pre = pre + dot(x2[2 * m + d], w2s[d])
+        act = rounded(gelu(pre))
         if 2 <= m < 8:
-            act_f, slope = gelu_both(pre[128:256])
-            act = rounded(jnp.concatenate([gelu(pre[0:128]), act_f], axis=0))
             act2[m - 2] = act.astype(BF)
-            sl2[m - 2] = slope
-        else:
-            act = rounded(gelu(pre))
+            sl2[m - 2] = pre[128:256]
         v = rounded(pool_cols(act[:, 0:128] + act[:, 128:256], 16) * 0.125)
         if m < 3:
             v = jnp.where(not_first, v, 0.0)
@@ -385,9 +386,9 @@
     def segment3(n):
         rows = [x3[2 * n + ky : 2 * n + ky + 2].reshape(256, 384) for ky in range(3)]
         pre = dot(jnp.concatenate(rows, axis=1), w3s[...]) + b3_ref[...] * 0.5
-        act, slope = both(pre, 64)
+        act = rounded(gelu(pre))
         act3[n] = act.astype(BF)
-        sl3[n] = slope
+        sl3[n] = jnp.concatenate([pre[64:128], pre[192:256]], axis=0)
         v = rounded(pool_cols(act[0:128] + act[128:256], 8) * 0.125)
         if n < 1:
             v = jnp.where(not_first, v, 0.0)
@@ -433,7 +434,7 @@
 
     def tap3(n, counted):
         act = act3[n].astype(F32).reshape(2, 2, 64, 256)
-        slope = sl3[n]
+        slope = slope_of(sl3[n])
         terms, grad = tap(
             act[:, 0].reshape(128, 256), act[:, 1].reshape(128, 256), l3_ref[...], lane_sum
         )
@@ -444,7 +445,7 @@
 
     def tap2(m, counted):
         act = act2[m - 2].astype(F32)
-        slope = sl2[m - 2]
+        slope = slope_of(sl2[m - 2])
         terms, grad = tap(act[0:128], act[128:256], lin2, sum_rows)
         if counted:
             parts[1] += fold(terms)

time: 36.7 us -> 36.2 us (0.986)
  Pallas kernels: 36 us -> 35.5 us
    pallas_call x1, Pallas kernels: 35.3 us -> 34.9 us  [on_device(): pl.pallas_call(body, out_shape=(v((1, 5), F32), v((1, 3, 16, 256), F32)),...]
where the time goes in v6:
time: 36.2 us
  Pallas kernels  35.5 us (98%)
  between operations  0.65 us (2%)
    pallas_call x1, Pallas kernels, on_device(): pl.pallas_call(body, out_shape=(v((1, 5), F32), v((1, 3, 16, 256), F32)),...  34.9 us

profile of v6, /device:TPU:1, one launch (start us, length us, event | category | flops | bytes accessed | tf_op | source)
XLA Modules:
  0.0 36.2 jit_solution(4712423121254336689)
XLA Ops:
  0.6 34.9 %whole_step.1 = (f32[1,5]{1,0:T(1,128)S(1)}, f32[1,3,16,256]{3,2,1,0:T(8,128)S(1)}) custom-call(bf16[1,3,16,256]{3,2,1,0:T(8,128)(2,1)} %real_hbm.1, bf16[1,3,16,256]{3,2,1,0:T(8,128)(2,1)} %fake_hbm.1, bf16[3,3,3,64]{3,2,1,0:T(4,128)(2,1)} %w1_hbm.1, bf16[576,128]{1,0:T(8,128)(2,1)} %bitcast.18, bf16[1152,256]{1,0:T(8,128)(2,1)} %bitcast.17, ...), custom_call_target="tpu_custom_call" | custom-call | tf_op jit(solution)/shard_map/whole_step/pallas_call | solution.py:652
  35.5 0.6 %hand_on.1 = (f32[1,5]{1,0:T(1,128)}, f32[1,3,16,256]{3,2,1,0:T(8,128)}) custom-call(f32[1,5]{1,0:T(1,128)S(1)} %get-tuple-element.6.losses_ref, f32[1,3,16,256]{3,2,1,0:T(8,128)S(1)} %get-tuple-element.7.grads_ref), custom_call_target="tpu_custom_call" | custom-call | tf_op jit(solution)/shard_map/hand_on/pallas_call | solution.py:663
